TPU v7x, 32 devices: a whole 2x2x4 slice. The times are simulated.
32 devices in a mesh: fsdp: 32 (over z, y, x, core).
Axes of the slice: x: 2, y: 2, z: 4, core: 2. Of those that a mesh axis runs over, the one named last changes fastest.
Arguments:
- inputs: bfloat16 [16384, 768], P('fsdp'), may hold values from -6 to 6
- cotangent: bfloat16 [16384, 768], P('fsdp'), may hold values from -6 to 6
- norm_gain: bfloat16 [2, 768], P(None, 'fsdp'), may hold values from 0.5 to 1.5
- in_w: bfloat16 [2, 768, 3248], P(None, 'fsdp'), may hold values from -0.21875 to 0.21875
- conv_w: bfloat16 [2, 4, 1664], P(None, None, 'fsdp'), may hold values from -3 to 3
- conv_b: bfloat16 [2, 1664], P(None, 'fsdp'), may hold values from -3 to 3
- dt_bias: float32 [2, 48], replicated, may hold values from -4.5 to -1
- a_log: float32 [2, 24], replicated, may hold values from -1.5 to 1
- skip: float32 [2, 24], replicated, may hold values from 0.5 to 1.5
- fc_d: bfloat16 [2, 1536, 24], P(None, 'fsdp'), may hold values from -0.15625 to 0.15625
- inner_gain: bfloat16 [2, 1536], P(None, 'fsdp'), may hold values from 0.5 to 1.5
- out_w: bfloat16 [2, 1536, 768], P(None, 'fsdp'), may hold values from -0.15625 to 0.15625
Outputs:
- output: float32 [16384, 768], P('fsdp')
- input_grad: float32 [16384, 768], P('fsdp')
- grad_norm_gain: float32 [2, 768], P(None, 'fsdp')
- grad_in_w: float32 [2, 768, 3248], P(None, 'fsdp')
- grad_conv_w: float32 [2, 4, 1664], P(None, None, 'fsdp')
- grad_conv_b: float32 [2, 1664], P(None, 'fsdp')
- grad_dt_bias: float32 [2, 48], replicated
- grad_a_log: float32 [2, 24], replicated
- grad_skip: float32 [2, 24], replicated
- grad_fc_d: float32 [2, 1536, 24], P(None, 'fsdp')
- grad_inner_gain: float32 [2, 1536], P(None, 'fsdp')
- grad_out_w: float32 [2, 1536, 768], P(None, 'fsdp')
All inputs are finite; a program needn't handle non-finite values.
Results may differ from a plain program's by a relative error of at most 0.012.
The roundings to bfloat16 on the way count: a program that leaves them out, or rounds other values in their place, can miss the bound.
Values may be sent and summed in bfloat16 or wider, within the bound.
No kernel may reach another device: no remote copies, remote signals or barrier semaphores. Data moves between devices by JAX's collectives and lax.ppermute only.
A program may use at most 384 MiB of HBM per device.

v0:
```python
import jax
import jax.numpy as jnp
from jax import lax
from jax.sharding import PartitionSpec as P

GROUP = 128


epsilon = 1e-05
highest = lax.Precision.HIGHEST


def rms_scale(values, gain):
    return values * lax.rsqrt(jnp.mean(values * values, axis=-1, keepdims=True) + epsilon) * gain


def ssd_scan(values, step_sizes, decay_rate, b_proj, c_proj, block_len):
    length, head_count, head_size = values.shape
    state_size = b_proj.shape[1]
    block_count = length // block_len
    rates = jnp.transpose(
        (step_sizes * decay_rate).reshape(block_count, block_len, head_count), (0, 2, 1)
    )
    weighted = (values * step_sizes[:, :, None]).reshape(
        block_count, block_len, head_count, head_size
    )
    b_blocks = b_proj.reshape(block_count, block_len, state_size)
    c_blocks = c_proj.reshape(block_count, block_len, state_size)
    cumulative = jnp.cumsum(rates, axis=2)
    gap_sums = cumulative[:, :, :, None] - cumulative[:, :, None, :]
    positions = jnp.arange(block_len)
    lower_mask = (positions[:, None] >= positions[None, :])[None, None, :, :]
    decay_kernel = jnp.where(lower_mask, jnp.exp(jnp.where(lower_mask, gap_sums, 0.0)), 0.0)
    scores = jnp.einsum("btn,bsn->bts", c_blocks, b_blocks, precision=highest)
    diag_out = jnp.einsum("bts,bhts,bshp->bthp", scores, decay_kernel, weighted, precision=highest)
    tail_decay = jnp.exp(cumulative[:, :, -1:] - cumulative)
    states = jnp.einsum("bhs,bshp,bsn->bhpn", tail_decay, weighted, b_blocks, precision=highest)
    block_decay = jnp.exp(cumulative[:, :, -1])

    def advance(running, item):
        fresh, factor = item
        return (running * factor[:, None, None] + fresh, running)

    start_state = jnp.zeros((head_count, head_size, state_size), jnp.float32)
    final_state, entering = lax.scan(advance, start_state, (states, block_decay))
    off_out = jnp.einsum(
        "btn,bhpn,bht->bthp", c_blocks, entering, jnp.exp(cumulative), precision=highest
    )
    return (diag_out + off_out).reshape(length, head_count, head_size)


def mixer(
    projected, conv_weight, conv_bias, steps_bias, decay_log, skip_gain, diag_weight, second_gain
):
    inner_width = second_gain.shape[0]
    width = conv_bias.shape[0]
    head_count = decay_log.shape[0]
    taps = conv_weight.shape[0]
    state_size = (width - inner_width) // 2
    length = projected.shape[0]
    gate_part = projected[:, :inner_width]
    conv_in = projected[:, inner_width : inner_width + width]
    raw_steps = projected[:, inner_width + width :]
    padded = jnp.pad(conv_in, ((taps - 1, 0), (0, 0)))
    conv_out = conv_bias + conv_weight[0] * padded[0:length]
    for offset in range(1, taps):
        conv_out = conv_out + conv_weight[offset] * padded[offset : offset + length]
    active = jax.nn.silu(conv_out)
    flat_values = active[:, :inner_width]
    values = flat_values.reshape(length, head_count, inner_width // head_count)
    b_proj = active[:, inner_width : inner_width + state_size]
    c_proj = active[:, inner_width + state_size :]
    steps_fwd = jax.nn.softplus(raw_steps[:, :head_count] + steps_bias[:head_count])
    steps_rev = jax.nn.softplus(raw_steps[:, head_count:] + steps_bias[head_count:])
    decay_rate = -jnp.exp(decay_log)
    forward_out = ssd_scan(values, steps_fwd, decay_rate, b_proj, c_proj, GROUP)
    reverse_out = jnp.flip(
        ssd_scan(
            jnp.flip(values, 0),
            jnp.flip(steps_rev, 0),
            decay_rate,
            jnp.flip(b_proj, 0),
            jnp.flip(c_proj, 0),
            GROUP,
        ),
        0,
    )
    shifted = jnp.pad(forward_out[:-1], ((1, 0), (0, 0), (0, 0))) + jnp.pad(
        reverse_out[1:], ((0, 1), (0, 0), (0, 0))
    )
    diagonal = skip_gain[None, :] + jnp.dot(flat_values, diag_weight, precision=highest)
    combined = shifted + diagonal[:, :, None] * values
    gated = combined.reshape(length, inner_width) * jax.nn.silu(gate_part)
    return rms_scale(gated, second_gain)


def layer_forward(current, full, head_part):
    first_gain, in_weight, conv_weight, conv_bias, second_gain, out_weight, diag_weight = full
    steps_bias, decay_log, skip_gain = head_part
    normed, norm_pull = jax.vjp(rms_scale, current, first_gain.astype(jnp.float32))
    lowered = normed.astype(jnp.bfloat16)
    projected = jnp.dot(lowered, in_weight, preferred_element_type=jnp.float32)
    mixed, mix_pull = jax.vjp(
        mixer,
        projected,
        conv_weight.astype(jnp.float32),
        conv_bias.astype(jnp.float32),
        steps_bias,
        decay_log,
        skip_gain,
        diag_weight.astype(jnp.float32),
        second_gain.astype(jnp.float32),
    )
    hidden = mixed.astype(jnp.bfloat16)
    branch = jnp.dot(hidden, out_weight, preferred_element_type=jnp.float32)
    return (current + branch, (lowered, hidden, norm_pull, mix_pull))


def layer_backward(upstream, full, saved):
    lowered, hidden, norm_pull, mix_pull = saved
    in_weight = full[1]
    out_weight = full[5]
    upstream_low = upstream.astype(jnp.bfloat16)
    grad_out_weight = jnp.einsum(
        "ti,td->id", hidden, upstream_low, preferred_element_type=jnp.float32
    )
    grad_hidden = jnp.einsum(
        "td,id->ti", upstream_low, out_weight, preferred_element_type=jnp.float32
    )
    (
        grad_proj,
        grad_conv_weight,
        grad_conv_bias,
        grad_steps,
        grad_decay,
        grad_skip,
        grad_diag,
        grad_second,
    ) = mix_pull(grad_hidden)
    proj_low = grad_proj.astype(jnp.bfloat16)
    grad_in_weight = jnp.einsum("td,tp->dp", lowered, proj_low, preferred_element_type=jnp.float32)
    grad_normed = jnp.einsum("tp,dp->td", proj_low, in_weight, preferred_element_type=jnp.float32)
    grad_input, grad_first = norm_pull(grad_normed)
    weight_part = (
        grad_first,
        grad_in_weight,
        grad_conv_weight,
        grad_conv_bias,
        grad_second,
        grad_out_weight,
        grad_diag,
    )
    return (upstream + grad_input, weight_part, (grad_steps, grad_decay, grad_skip))


def shards(
    inputs,
    cotangent,
    norm_gain,
    in_w,
    conv_w,
    conv_b,
    dt_bias,
    a_log,
    skip,
    fc_d,
    inner_gain,
    out_w,
):
    layer_total = in_w.shape[0]
    current = inputs.astype(jnp.float32)
    layer_inputs = []
    kept_state = []
    for number in range(layer_total):
        full = (
            lax.all_gather(norm_gain[number], "fsdp", axis=0, tiled=True),
            lax.all_gather(in_w[number], "fsdp", axis=0, tiled=True),
            lax.all_gather(conv_w[number], "fsdp", axis=1, tiled=True),
            lax.all_gather(conv_b[number], "fsdp", axis=0, tiled=True),
            lax.all_gather(inner_gain[number], "fsdp", axis=0, tiled=True),
            lax.all_gather(out_w[number], "fsdp", axis=0, tiled=True),
            lax.all_gather(fc_d[number], "fsdp", axis=0, tiled=True),
        )
        layer_inputs.append(current)
        current, saved = layer_forward(
            current, full, (dt_bias[number], a_log[number], skip[number])
        )
        kept_state.append((full, saved))
    upstream = cotangent.astype(jnp.float32)
    weight_grads = [None] * layer_total
    head_grads = [None] * layer_total
    for number in reversed(range(layer_total)):
        full = (
            lax.all_gather(norm_gain[number], "fsdp", axis=0, tiled=True),
            lax.all_gather(in_w[number], "fsdp", axis=0, tiled=True),
            lax.all_gather(conv_w[number], "fsdp", axis=1, tiled=True),
            lax.all_gather(conv_b[number], "fsdp", axis=0, tiled=True),
            lax.all_gather(inner_gain[number], "fsdp", axis=0, tiled=True),
            lax.all_gather(out_w[number], "fsdp", axis=0, tiled=True),
            lax.all_gather(fc_d[number], "fsdp", axis=0, tiled=True),
        )
        recomputed, saved = layer_forward(
            layer_inputs[number], full, (dt_bias[number], a_log[number], skip[number])
        )
        upstream, local_grads, head_grads[number] = layer_backward(upstream, full, saved)
        first_part, in_part, conv_part, bias_part, second_part, out_part, diag_part = local_grads
        weight_grads[number] = (
            lax.psum_scatter(first_part, "fsdp", scatter_dimension=0, tiled=True),
            lax.psum_scatter(in_part, "fsdp", scatter_dimension=0, tiled=True),
            lax.psum_scatter(conv_part, "fsdp", scatter_dimension=1, tiled=True),
            lax.psum_scatter(bias_part, "fsdp", scatter_dimension=0, tiled=True),
            lax.psum_scatter(second_part, "fsdp", scatter_dimension=0, tiled=True),
            lax.psum_scatter(out_part, "fsdp", scatter_dimension=0, tiled=True),
            lax.psum_scatter(diag_part, "fsdp", scatter_dimension=0, tiled=True),
        )
    stacked = [
        jnp.stack([weight_grads[number][member] for number in range(layer_total)])
        for member in range(7)
    ]
    steps_local = jnp.stack([head_grads[number][0] for number in range(layer_total)])
    decay_local = jnp.stack([head_grads[number][1] for number in range(layer_total)])
    skip_local = jnp.stack([head_grads[number][2] for number in range(layer_total)])
    steps_total, decay_total, skip_total = lax.psum((steps_local, decay_local, skip_local), "fsdp")
    return (
        current,
        upstream,
        stacked[0],
        stacked[1],
        stacked[2],
        stacked[3],
        steps_total,
        decay_total,
        skip_total,
        stacked[6],
        stacked[4],
        stacked[5],
    )


def solution(mesh):
    return jax.shard_map(
        shards,
        mesh=mesh,
        in_specs=(
            P("fsdp", None),
            P("fsdp", None),
            P(None, "fsdp"),
            P(None, "fsdp", None),
            P(None, None, "fsdp"),
            P(None, "fsdp"),
            P(),
            P(),
            P(),
            P(None, "fsdp", None),
            P(None, "fsdp"),
            P(None, "fsdp", None),
        ),
        out_specs=(
            P("fsdp", None),
            P("fsdp", None),
            P(None, "fsdp"),
            P(None, "fsdp", None),
            P(None, None, "fsdp"),
            P(None, "fsdp"),
            P(),
            P(),
            P(),
            P(None, "fsdp", None),
            P(None, "fsdp"),
            P(None, "fsdp", None),
        ),
        check_vma=False,
    )
```

profile of v0, /device:TPU:0, one launch (start us, length us, event | category | flops | bytes accessed | tf_op | source)
XLA Modules:
  0.0 2116.5 jit_solution(2690165319581879344)
XLA Ops:
  16.2 42.3 %all-reduce.73 = (bf16[768]{0:T(1024)(128)(2,1)S(1)}, bf16[1664]{0:T(1024)(128)(2,1)S(1)}, bf16[1536]{0:T(1024)(128)(2,1)S(1)}, bf16[768]{0:T(1024)(128)(2,1)S(1...) all-reduce(bf16[768]{0:T(1024)(128)(2,1)S(1)} %dynamic-update-slice, ...), channel_id=2, replica_groups=mesh['fsdp'=32] {'fsdp'}, use_global_device_ids=true, to_apply=%add.58 | all-reduce | flops 7936 | bytes 31744
  60.8 43.7 %all-gather.3 = bf16[1,4,1664]{1,0,2:T(2,128)(2,1)S(1)} all-gather(bf16[1,4,52]{1,0,2:T(2,128)(2,1)S(1)} %copy.788), channel_id=5, replica_groups=mesh['fsdp'=32] {'fsdp'}, dimensions={2}, use_global_device_ids=true | all-gather | bytes 13728 | tf_op jit(solution)/shard_map/all_gather | solution.py:178
  105.4 34.5 %slice_reduce_fusion.7 = (f32[1664]{0:T(1024)S(1)}, f32[1664]{0:T(1024)S(1)}, f32[1664]{0:T(1024)S(1)}, f32[1664]{0:T(1024)S(1)}) fusion(f32[1,4,1664]{1,0,2:T(1,128)S(1)} %convert_element_type.108), kind=kLoop, calls=%fused_computation.467 | loop fusion | bytes 53248 | tf_op jit(solution)/shard_map/jvp()/slice | solution.py:65
  140.1 40.1 %all-gather.4 = bf16[1,1536,24]{2,0,1:T(2,128)(2,1)S(1)} all-gather(bf16[1,48,24]{2,0,1:T(2,128)(2,1)S(1)} %copy.789), channel_id=6, replica_groups=mesh['fsdp'=32] {'fsdp'}, dimensions={1}, use_global_device_ids=true | all-gather | bytes 76032 | tf_op jit(solution)/shard_map/all_gather | solution.py:182
  183.6 41.3 %all-gather.10 = bf16[1,4,1664]{1,0,2:T(2,128)(2,1)S(1)} all-gather(bf16[1,4,52]{1,0,2:T(2,128)(2,1)S(1)} %copy.790), channel_id=12, replica_groups=mesh['fsdp'=32] {'fsdp'}, dimensions={2}, use_global_device_ids=true | all-gather | bytes 13728 | tf_op jit(solution)/shard_map/all_gather | solution.py:178
  225.8 35.1 %slice_reduce_fusion.3 = (f32[1664]{0:T(1024)}, f32[1664]{0:T(1024)}, f32[1664]{0:T(1024)}, f32[1664]{0:T(1024)}) fusion(f32[1,4,1664]{1,0,2:T(1,128)S(1)} %convert_element_type.112), kind=kLoop, calls=%fused_computation.463 | loop fusion | bytes 53248 | tf_op jit(solution)/shard_map/jvp()/slice | solution.py:65
  261.6 40.1 %all-gather.11 = bf16[1,1536,24]{2,0,1:T(2,128)(2,1)S(1)} all-gather(bf16[1,48,24]{2,0,1:T(2,128)(2,1)S(1)} %copy.791), channel_id=13, replica_groups=mesh['fsdp'=32] {'fsdp'}, dimensions={1}, use_global_device_ids=true | all-gather | bytes 76032 | tf_op jit(solution)/shard_map/all_gather | solution.py:182
  358.8 9.6 while.197
  373.6 13.1 fusion.44
  404.0 9.4 while.196
  415.3 15.5 fusion.50
  442.2 11.8 while.189
  470.3 12.0 while.188
  499.1 8.2 add_add_fusion.2
  507.4 8.8 multiply_reduce_fusion.22
  535.4 6.2 fusion.72
  576.3 17.1 while.193
  593.5 13.8 fusion.32
  633.2 9.1 while.191
  657.9 14.4 fusion.38
  679.2 9.0 while.190
  699.5 9.1 while.192
  718.9 8.4 add_add_fusion.3
  737.1 6.7 multiply_reduce_fusion.18
  774.4 13.8 while.195
  788.2 6.7 multiply_reduce_fusion.12
  807.1 6.4 fusion.298
  813.5 8.5 fusion.102
  824.2 21.6 %while.194 = (s32[]{:T(128)}, f32[24,64,64]{2,1,0:T(8,128)}, f32[4,24,64,64]{3,2,1,0:T(8,128)}, f32[4,24]{1,0:T(4,128)S(1)}, f32[4,24,64,64]{3,2,1,0:T(8,128)}, ...) while((s32[]{:T(128)}, f32[24,64,64]{2,1,0:T(8,128)}, ...), condition=%wide.region_26.28_spmd.clone, body=%wide.region_24.27_spmd.clone.sunk | while | flops 589804 | bytes 3146452 | solution.py:45
  845.8 8.1 fusion.301
  857.6 12.2 fusion.90
  869.8 6.9 fusion.103
  879.7 7.0 rev.89
  886.8 17.2 fusion.24
  914.7 6.2 fusion.81
  923.7 11.1 multiply_reduce_fusion.2
  934.8 6.5 broadcast_multiply_fusion
  941.3 9.2 fusion.61
  979.4 7.8 pad_add_fusion.3
  987.2 7.4 multiply_reduce_fusion.28
  1036.3 13.6 while.199
  1050.0 7.0 multiply_reduce_fusion.8
  1069.2 6.5 fusion.295
  1075.7 8.4 fusion.96
  1086.3 13.8 while.198
  1100.2 9.1 fusion.302
  1113.2 12.1 fusion.93
  1125.4 7.2 fusion.97
  1135.4 7.1 rev.95
  1142.5 17.2 fusion.18
  1170.6 6.2 fusion.78
  1179.6 11.6 multiply_reduce_fusion.6
  1197.4 9.3 fusion.65
  1245.5 7.8 pad_add_fusion
  1255.1 7.5 fusion.229
  1285.6 9.9 fusion.442
  1296.5 9.8 fusion.305
  1315.7 70.7 %all-reduce.76.cloned.1.call-done = (f32[768]{0:T(1024)}, f32[768]{0:T(1024)}, f32[4,1664]{1,0:T(4,128)}, f32[4,1664]{1,0:T(4,128)}, f32[1664]{0:T(1024)}, /*ind...) async-done(((f32[768]{0:T(1024)}, f32[768]{0:T(1024)}, f32[4,1664]{1,0:T(4,128)}, ...) | async-done | bytes 85776
  1394.8 93.9 %reduce-scatter.23.cloned.1.call-done = f32[48,24]{1,0:T(8,128)} async-done(((f32[1536,24]{1,0:T(8,128)}), f32[48,24]{1,0:T(8,128)}) %reduce-scatter.23.cloned.1.call-update) | async-done | bytes 4624
  1489.4 99.7 %reduce-scatter.21.cloned.1.call-done = f32[48,24]{1,0:T(8,128)} async-done(((f32[1536,24]{1,0:T(8,128)}), f32[48,24]{1,0:T(8,128)}) %reduce-scatter.21.cloned.1.call-update) | async-done | bytes 4624
  1590.6 111.0 %reduce-scatter.19.cloned.1.call-done = f32[48,768]{1,0:T(8,128)} async-done(((f32[1536,768]{1,0:T(8,128)}), f32[48,768]{1,0:T(8,128)}) %reduce-scatter.19.cloned.1.call-update) | async-done | bytes 147472 | tf_op jit(solution)/shard_map/reduce_scatter | solution.py:213
  1701.5 111.6 %reduce-scatter.17.cloned.1.call-done = f32[48,768]{1,0:T(8,128)} async-done(((f32[1536,768]{1,0:T(8,128)}), f32[48,768]{1,0:T(8,128)}) %reduce-scatter.17.cloned.1.call-update) | async-done | bytes 147472 | tf_op jit(solution)/shard_map/reduce_scatter | solution.py:213
  1814.8 143.7 %reduce-scatter.15.cloned.1.call-done = f32[24,3248]{1,0:T(8,128)} async-done(((f32[768,3248]{1,0:T(8,128)}), f32[24,3248]{1,0:T(8,128)}) %reduce-scatter.15.cloned.1.call-update) | async-done | bytes 311824 | tf_op jit(solution)/shard_map/reduce_scatter | solution.py:209
  1958.5 145.5 %reduce-scatter.13.cloned.1.call-done = f32[24,3248]{1,0:T(8,128)} async-done(((f32[768,3248]{1,0:T(8,128)}), f32[24,3248]{1,0:T(8,128)}) %reduce-scatter.13.cloned.1.call-update) | async-done | bytes 311824 | tf_op jit(solution)/shard_map/reduce_scatter | solution.py:209
  (1123 shorter events, 690.9 us)
Async XLA Ops:
  7.2 297.3 %all-gather.19.cloned.1.call-start = ((), (), s32[]{:S(2)}) async-start(), calls=%async_computation.10 | async-start | bytes 5271552 | tf_op jit(solution)/shard_map/all_gather | solution.py:177
  9.0 507.2 %all-gather.21.cloned.1.call-start = ((), (), s32[]{:S(2)}) async-start(), calls=%async_computation.11 | async-start | bytes 2433024 | tf_op jit(solution)/shard_map/all_gather | solution.py:181
  10.6 511.3 %all-gather.23.cloned.1.call-start = ((), (), s32[]{:S(2)}) async-start(), calls=%async_computation.12 | async-start | bytes 5271552 | tf_op jit(solution)/shard_map/all_gather | solution.py:177
  11.4 719.9 %all-gather.25.cloned.1.call-start = ((), (), s32[]{:S(2)}) async-start(), calls=%async_computation.13 | async-start | bytes 2433024 | tf_op jit(solution)/shard_map/all_gather | solution.py:181
  11.9 1374.4 %all-reduce.76.cloned.1.call-start = ((), (), s32[]{:S(2)}) async-start(), calls=%async_computation.16 | async-start | bytes 194560
  58.5 245.9 %copy-start.250 = (f32[768]{0:T(1024)}, f32[768]{0:T(1024)S(1)}, u32[]{:S(2)}) copy-start(f32[768]{0:T(1024)S(1)} %convert_element_type.114) | copy-start | bytes 9220
  59.9 80.0 %copy-start.258 = (bf16[2,48,24]{1,2,0:T(8,128)(2,1)S(1)}, bf16[2,48,24]{1,2,0:T(8,128)(2,1)}, u32[]{:S(2)}) copy-start(bf16[2,48,24]{1,2,0:T(8,128)(2,1)} %param.46) | copy-start | bytes 13828
  59.9 244.5 %copy-start.259 = (f32[512]{0:T(512)}, f32[512]{0:T(512)S(1)}, u32[]{:S(2)}) copy-start(f32[512]{0:T(512)S(1)} %fusion.430) | copy-start | bytes 6148
  104.5 77.2 %copy-start.290 = (f32[2,24]{1,0:T(2,128)S(1)}, f32[2,24]{1,0:T(2,128)}, u32[]{:S(2)}) copy-start(f32[2,24]{1,0:T(2,128)} %param.45) | copy-start | bytes 580
  139.9 178.4 %copy-start.219 = (f32[1664]{0:T(1024)}, f32[1664]{0:T(1024)S(1)}, u32[]{:S(2)}) copy-start(f32[1664]{0:T(1024)S(1)} %get-tuple-element.1142) | copy-start | bytes 19972
  139.9 178.4 %copy-start.220 = (f32[1664]{0:T(1024)}, f32[1664]{0:T(1024)S(1)}, u32[]{:S(2)}) copy-start(f32[1664]{0:T(1024)S(1)} %get-tuple-element.1143) | copy-start | bytes 19972
  139.9 178.4 %copy-start.221 = (f32[1664]{0:T(1024)}, f32[1664]{0:T(1024)S(1)}, u32[]{:S(2)}) copy-start(f32[1664]{0:T(1024)S(1)} %get-tuple-element.1144) | copy-start | bytes 19972
  139.9 178.4 %copy-start.222 = (f32[1664]{0:T(1024)}, f32[1664]{0:T(1024)S(1)}, u32[]{:S(2)}) copy-start(f32[1664]{0:T(1024)S(1)} %get-tuple-element.1145) | copy-start | bytes 19972
  224.9 79.0 %copy-start.279 = (f32[2,48]{1,0:T(2,128)S(1)}, f32[2,48]{1,0:T(2,128)}, u32[]{:S(2)}) copy-start(f32[2,48]{1,0:T(2,128)} %param.43) | copy-start | bytes 1156
  224.9 79.0 %copy-start.280 = (f32[2,24]{1,0:T(2,128)S(1)}, f32[2,24]{1,0:T(2,128)}, u32[]{:S(2)}) copy-start(f32[2,24]{1,0:T(2,128)} %param.44) | copy-start | bytes 580
  224.9 79.6 %copy-start.90 = (bf16[512,768]{1,0:T(8,128)(2,1)S(1)}, bf16[512,768]{1,0:T(8,128)(2,1)}, u32[]{:S(2)}) copy-start(bf16[512,768]{1,0:T(8,128)(2,1)} %param.37) | copy-start | bytes 2359300
  313.3 60.2 %copy-start.97 = (f32[512,24]{0,1:T(8,128)}, f32[512,24]{0,1:T(8,128)S(1)}, u32[]{:S(2)}) copy-start(f32[512,24]{0,1:T(8,128)S(1)} %rev.76) | copy-start | bytes 147460
  314.5 59.0 %copy-start.109 = (f32[4,24,128]{2,1,0:T(8,128)}, f32[4,24,128]{2,1,0:T(8,128)S(1)}, u32[]{:S(2)}) copy-start(f32[4,24,128]{2,1,0:T(8,128)S(1)} %reduce_window_sum.62) | copy-start | bytes 147460
  325.6 17.8 copy-start.5
  326.1 108.6 %copy-start.105 = (f32[4,128,64]{1,0,2:T(4,128)}, f32[4,128,64]{1,0,2:T(4,128)S(1)}, u32[]{:S(2)}) copy-start(f32[4,128,64]{1,0,2:T(4,128)S(1)} %reshape.583) | copy-start | bytes 393220
  330.8 123.1 %copy-start.111 = (f32[4,128,64]{1,0,2:T(4,128)}, f32[4,128,64]{1,0,2:T(4,128)S(1)}, u32[]{:S(2)}) copy-start(f32[4,128,64]{1,0,2:T(4,128)S(1)} %reshape.582) | copy-start | bytes 393220
  336.0 78.6 %copy-start.107 = (f32[4,24,128]{2,1,0:T(8,128)}, f32[4,24,128]{2,1,0:T(8,128)S(1)}, u32[]{:S(2)}) copy-start(f32[4,24,128]{2,1,0:T(8,128)S(1)} %reduce_window_sum.58) | copy-start | bytes 147460
  373.6 13.1 copy-start.51
  373.6 13.1 copy-start.131
  397.3 17.3 copy-start.155
  528.4 13.2 copy-start.49
  543.4 17.6 copy-start.8
  566.4 27.0 %copy-start.3 = (f32[512,24,64]{0,2,1:T(8,128)}, f32[512,24,64]{0,2,1:T(8,128)S(1)}, u32[]{:S(2)}) copy-start(f32[512,24,64]{0,2,1:T(8,128)S(1)} %rev.83) | copy-start | bytes 9437188
  576.3 17.2 copy-start.196
  593.5 13.9 copy-start.283
  593.5 13.9 copy-start.33
  593.5 13.9 copy-start.115
  657.9 14.4 copy-start.150
  657.9 14.4 copy-start.127
  657.9 14.4 copy-start.174
  697.4 19.5 copy-start.192
  774.4 13.8 copy-start.128
  774.4 13.8 copy-start.158
  824.2 21.6 %copy-start.4 = (f32[512,24,64]{0,2,1:T(8,128)S(1)}, f32[512,24,64]{0,2,1:T(8,128)}, u32[]{:S(2)}) copy-start(f32[512,24,64]{0,2,1:T(8,128)} %copy-done.3) | copy-start | bytes 9437188
  824.2 21.6 %copy-start.163 = (f32[4,128,24]{1,2,0:T(8,128)S(1)}, f32[4,128,24]{1,2,0:T(8,128)}, u32[]{:S(2)}) copy-start(f32[4,128,24]{1,2,0:T(8,128)} %get-tuple-element.1412) | copy-start | bytes 147460
  857.6 12.2 copy-start.148
  886.8 17.3 copy-start.124
  886.8 17.3 copy-start.176
  886.8 21.5 %copy-start.123 = (f32[512,64]{0,1:T(8,128)S(1)}, f32[512,64]{0,1:T(8,128)}, u32[]{:S(2)}) copy-start(f32[512,64]{0,1:T(8,128)} %copy-done.122) | copy-start | bytes 393220
  920.9 20.4 slice-start.2
  923.7 17.5 slice-start.3
  1036.3 13.7 copy-start.126
  1036.3 13.7 copy-start.156
  1086.3 13.9 copy-start.98
  1086.3 13.9 copy-start.161
  1113.2 12.2 copy-start.143
  1142.5 17.2 copy-start.121
  1142.5 17.2 copy-start.177
  1142.5 21.4 %copy-start.120 = (f32[512,64]{0,1:T(8,128)S(1)}, f32[512,64]{0,1:T(8,128)}, u32[]{:S(2)}) copy-start(f32[512,64]{0,1:T(8,128)} %copy-done.119) | copy-start | bytes 393220
  1176.8 20.5 slice-start
  1179.6 17.7 slice-start.1
  1216.4 12.2 copy-start.232
  1216.4 12.2 copy-start.54
  1262.7 225.9 %reduce-scatter.23.cloned.1.call-start = ((), (), s32[]{:S(2)}) async-start(), calls=%async_computation.15 | async-start | bytes 811008
  1266.3 322.8 %reduce-scatter.21.cloned.1.call-start = ((), (), s32[]{:S(2)}) async-start(), calls=%async_computation.14 | async-start | bytes 811008
  1272.3 429.2 %reduce-scatter.19.cloned.1.call-start = ((), (), s32[]{:S(2)}) async-start(), calls=%async_computation.9 | async-start | bytes 4866048 | tf_op jit(solution)/shard_map/reduce_scatter | solution.py:213
  1277.2 536.0 %reduce-scatter.17.cloned.1.call-start = ((), (), s32[]{:S(2)}) async-start(), calls=%async_computation.8 | async-start | bytes 4866048 | tf_op jit(solution)/shard_map/reduce_scatter | solution.py:213
  1284.2 674.3 %reduce-scatter.15.cloned.1.call-start = ((), (), s32[]{:S(2)}) async-start(), calls=%async_computation.7 | async-start | bytes 10543104 | tf_op jit(solution)/shard_map/reduce_scatter | solution.py:209
  1295.4 808.6 %reduce-scatter.13.cloned.1.call-start = ((), (), s32[]{:S(2)}) async-start(), calls=%async_computation.6 | async-start | bytes 10543104 | tf_op jit(solution)/shard_map/reduce_scatter | solution.py:209
  (242 other events, 1327.4 us)
Sparse Core Ops, SparseCore 0:
  11.5 70.0 all-gather.18
  84.4 56.9 all-gather.20
  144.9 67.7 all-gather.22
  215.5 56.6 all-gather.24
  1262.8 123.5 all-reduce.75
  1392.1 96.4 reduce-scatter.22
  1494.5 94.5 reduce-scatter.20
  1595.5 105.9 reduce-scatter.18
  1707.0 106.0 reduce-scatter.16
  1820.0 138.4 reduce-scatter.14
  1965.5 138.4 reduce-scatter.12
where the time goes:
time: 2130 us; the launch traced here: 2120 us
  waiting for transfers between devices  777 us (36%)
  matrix products  408 us (19%)
  other arithmetic  369 us (17%)
  local copies, waits for them, and re-layouts  334 us (16%)
  blocking collectives  208 us (10%)
    reduce_scatter x2, waiting for transfers between devices, shards(): lax.psum_scatter(in_part, 'fsdp', scatter_dimension=0, tiled=True)  289 us
    unnamed x14, waiting for transfers between devices  266 us
    reduce_scatter x2, waiting for transfers between devices, shards(): lax.psum_scatter(out_part, 'fsdp', scatter_dimension=0, tiled=True)  223 us
    dot_general x12, matrix products, ssd_scan(): jnp.einsum('bts,bhts,bshp->bthp', scores, decay_kernel, weighted, precisi...  147 us
    all_gather x2, blocking collectives, shards(): lax.all_gather(conv_w[number], 'fsdp', axis=1, tiled=True)  85 us
    dot_general x16, matrix products, ssd_scan(): jnp.einsum('btn,bhpn,bht->bthp', c_blocks, entering, jnp.exp(cumulative),...  80.5 us
    all_gather x2, blocking collectives, shards(): lax.all_gather(fc_d[number], 'fsdp', axis=0, tiled=True)  80.2 us
    dot_general x14, matrix products, ssd_scan(): jnp.einsum('bhs,bshp,bsn->bhpn', tail_decay, weighted, b_blocks, precisio...  78 us
  transfers between devices with their start and end apart: 11, of which 7 were waited for; matrix products, arithmetic and copies ran while one was open for 26% of the time, Pallas kernels for 0%

commit v1 on v0

v1 whole, which is shorter than its diff:
```python
import functools

import jax
import jax.numpy as jnp
from jax import lax
from jax.experimental import pallas as pl
from jax.experimental.pallas import tpu as pltpu
from jax.sharding import PartitionSpec as P

Q = 128
EPS = 1e-05
F32 = jnp.float32
BF16 = jnp.bfloat16
NN = (((1,), (0,)), ((), ()))
NT = (((1,), (1,)), ((), ()))
TN = (((0,), (0,)), ((), ()))
MIB = 1024 * 1024


def mm(a, b, dims=NN):
    return lax.dot_general(
        a.astype(BF16), b.astype(BF16), dims, preferred_element_type=F32
    )


def split2(a):
    high = a.astype(BF16)
    return high, (a - high.astype(F32)).astype(BF16)


def mm_left(a, b, dims=NN):
    high, low = split2(a)
    return mm(high, b, dims) + mm(low, b, dims)


def mm3(a, b, dims=NN):
    ah, al = split2(a)
    bh, bl = split2(b)
    return mm(ah, bh, dims) + (mm(ah, bl, dims) + mm(al, bh, dims))


def exact(a, b, dims=NN):
    return lax.dot_general(
        a, b, dims, preferred_element_type=F32, precision=lax.Precision.HIGHEST
    )


def iota(shape, axis):
    return lax.broadcasted_iota(jnp.int32, shape, axis)


def sigmoid(v):
    return 1.0 / (1.0 + jnp.exp(-v))


def rows_of(b, size=Q):
    return pl.ds(pl.multiple_of(b * Q, Q), size)


def lanes_of(j, size=Q):
    return pl.ds(pl.multiple_of(j * size, size), size)


def spread_matrix(ref, heads, width):
    shape = ref.shape
    ref[...] = (iota(shape, 1) // width == iota(shape, 0) % heads).astype(F32).astype(BF16)


def spread(values, matrix):
    high = values.astype(BF16)
    rest = values - high.astype(F32)
    middle = rest.astype(BF16)
    low = (rest - middle.astype(F32)).astype(BF16)
    stacked = jnp.concatenate(
        [high.astype(F32), middle.astype(F32), low.astype(F32)], axis=0
    ).T.astype(BF16)
    return mm(stacked, matrix)


def head_sums(matrix, values):
    high, low = split2(values)
    return mm(matrix, high, NT) + mm(matrix, low, NT)


def step_terms(raw_t, bias, rate, heads):
    shifted = raw_t + bias
    steps = jnp.maximum(shifted, 0.0) + jnp.log1p(jnp.exp(-jnp.abs(shifted)))
    decay = steps * rate
    r, c = iota((Q, 2 * Q), 0), iota((Q, 2 * Q), 1)
    upto = jnp.where(c < Q, (r <= c).astype(F32), (r < c - Q).astype(F32))
    sums = exact(decay, upto)
    inc, exc = sums[:, :Q], sums[:, Q:]
    log_steps = jnp.maximum(jnp.log(steps), -200.0)
    return dict(
        shifted=shifted,
        steps=steps,
        f=inc[:heads],
        fe=exc[:heads],
        ri=inc[heads:],
        re=exc[heads:],
        row_f=inc[:heads] - log_steps[:heads],
        row_r=exc[heads:] + log_steps[heads:],
        f_last=jnp.sum(decay[:heads], axis=1, keepdims=True),
        r_last=jnp.sum(decay[heads:], axis=1, keepdims=True),
    )


def weights_of(terms, heads):
    ef = jnp.exp(terms["fe"])
    er = jnp.exp(jnp.minimum(terms["r_last"] - terms["ri"], 0.0))
    wf = jnp.exp(jnp.minimum(terms["f_last"] - terms["f"], 0.0)) * terms["steps"][:heads]
    wr = jnp.exp(terms["re"]) * terms["steps"][heads:]
    return ef, er, wf, wr


def conv_tile(ci_ref, cw_ref, cb_ref, b, j):
    window = ci_ref[rows_of(b, Q + 8), lanes_of(j)]
    taps = cw_ref.shape[0]
    total = cb_ref[:, lanes_of(j)].astype(F32)
    for k in range(taps):
        start = 8 - (taps - 1) + k
        total = total + cw_ref[k : k + 1, lanes_of(j)].astype(F32) * window[start : start + Q]
    return total


def activate(ci_ref, cw_ref, cb_ref, xs_ref, bc_ref, blocks, inner):
    tiles = inner // Q

    def block(b, carry):
        def tile(j, carry):
            v = conv_tile(ci_ref, cw_ref, cb_ref, b, j)
            xs_ref[rows_of(b), lanes_of(j)] = v / (1.0 + jnp.exp(-v))
            return carry

        lax.fori_loop(0, tiles, tile, 0)
        v = conv_tile(ci_ref, cw_ref, cb_ref, b, tiles)
        bc_ref[pl.ds(pl.multiple_of(b * Q + 8, 8), Q), :] = v / (1.0 + jnp.exp(-v))
        return carry

    zero8 = jnp.zeros((8, Q), F32)
    bc_ref[0:8, :] = zero8
    bc_ref[blocks * Q + 8 : blocks * Q + 16, :] = zero8
    lax.fori_loop(0, blocks, block, 0)


def shifted_bc(bc_ref, b):
    window = bc_ref[rows_of(b, Q + 16), :]
    state = Q // 2
    here = window[8 : 8 + Q]
    return here[:, :state], window[7 : 7 + Q][:, state:], window[9 : 9 + Q][:, state:]


def pair_diagonal(tile):
    lane = iota(tile.shape, 1)
    zero = jnp.zeros_like(tile)
    return jnp.concatenate(
        [jnp.where(lane < Q // 2, tile, zero), jnp.where(lane >= Q // 2, tile, zero)], axis=0
    )


def forward_mix_kernel(
    x_ref, g_ref, wb_ref, cw_ref, cb_ref, dtb_ref, alog_ref, skip_ref, fcd_ref,
    u_ref, ci_ref, rawt_ref, m_ref, s_ref, z_ref,
    xs_ref, bc_ref, wide_ref, narrow_ref, colf_ref, colr_ref, rowf_ref, rowr_ref,
):
    tokens, inner = m_ref.shape
    heads = alog_ref.shape[0]
    channels = cb_ref.shape[1]
    blocks = tokens // Q
    state = Q // 2
    ci_ref[0:8, :] = jnp.zeros((8, channels), F32)

    def project(b, carry):
        x = x_ref[rows_of(b), :].astype(F32)
        scale = lax.rsqrt(jnp.mean(x * x, axis=-1, keepdims=True) + EPS)
        u = (x * scale * g_ref[...].astype(F32)).astype(BF16)
        u_ref[rows_of(b), :] = u
        here = mm(u, wb_ref[...])
        ci_ref[pl.ds(pl.multiple_of(b * Q + 8, 8), Q), :] = here[:, :channels]
        raw = jnp.concatenate(
            [here[:, channels:], jnp.zeros((Q, Q - 2 * heads), F32)], axis=1
        )
        rawt_ref[:, rows_of(b)] = raw.T[: 2 * heads]
        return carry

    lax.fori_loop(0, blocks, project, 0)
    activate(ci_ref, cw_ref, cb_ref, xs_ref, bc_ref, blocks, inner)
    spread_matrix(wide_ref, heads, Q)
    spread_matrix(narrow_ref, heads, inner // heads)
    rate_one = -jnp.exp(alog_ref[...])
    rate = jnp.concatenate([rate_one, rate_one], axis=0)
    s_ref[0] = jnp.zeros((state, inner), F32)
    z_ref[blocks - 1] = jnp.zeros((state, inner), F32)

    def states(b, carry):
        terms = step_terms(rawt_ref[:, rows_of(b)], dtb_ref[...], rate, heads)
        ef, er, wf, wr = weights_of(terms, heads)
        x = xs_ref[rows_of(b), :]
        bmat, _, _ = shifted_bc(bc_ref, b)
        bt = bmat.T

        @pl.when(b < blocks - 1)
        def _():
            fresh = mm_left(bt, spread(wf, narrow_ref[...]) * x)
            factor = jnp.broadcast_to(jnp.exp(terms["f_last"]), (heads, Q))
            s_ref[b + 1] = s_ref[b] * spread(factor, narrow_ref[...])[0:1] + fresh

        @pl.when(b > 0)
        def _():
            z_ref[b - 1] = mm_left(bt, spread(wr, narrow_ref[...]) * x)

        return carry

    lax.fori_loop(0, blocks, states, 0)

    def later(i, carry):
        b = blocks - 2 - i
        terms = step_terms(rawt_ref[:, rows_of(b + 1)], dtb_ref[...], rate, heads)
        factor = jnp.broadcast_to(jnp.exp(terms["r_last"]), (heads, Q))
        z_ref[b] = z_ref[b] + z_ref[b + 1] * spread(factor, narrow_ref[...])[0:1]
        return carry

    lax.fori_loop(0, blocks - 1, later, 0)

    def mix(b, carry):
        terms = step_terms(rawt_ref[:, rows_of(b)], dtb_ref[...], rate, heads)
        ef, er, wf, wr = weights_of(terms, heads)
        colf_ref[...] = spread(terms["fe"], wide_ref[...])
        colr_ref[...] = spread(terms["ri"], wide_ref[...])
        rowf_ref[...] = terms["row_f"]
        rowr_ref[...] = terms["row_r"]
        x = xs_ref[rows_of(b), :]
        bmat, cdn, cup = shifted_bc(bc_ref, b)
        diag = head_sums(fcd_ref[...].astype(F32), x) + skip_ref[...]
        off = spread(diag, narrow_ref[...]) * x
        off = off + spread(ef, narrow_ref[...]) * mm_left(cdn, s_ref[b])
        off = off + spread(er, narrow_ref[...]) * mm_left(cup, z_ref[b])
        m_ref[rows_of(b), :] = off
        t, s = iota((Q, Q), 0), iota((Q, Q), 1)
        lower = s < t
        gram = jnp.where(lower, exact(cdn, bmat, NT), exact(cup, bmat, NT))
        gram = jnp.where(s == t, 0.0, gram)

        def pair(p, carry):
            kernels = []
            for j in range(2):
                h = 2 * p + j
                gaps = jnp.where(
                    lower,
                    colf_ref[:, lanes_of(h)] - rowf_ref[pl.ds(h, 1), :],
                    rowr_ref[pl.ds(h, 1), :] - colr_ref[:, lanes_of(h)],
                )
                kernels.append((gram * jnp.exp(jnp.minimum(gaps, 60.0))).astype(BF16))
            tile = xs_ref[rows_of(b), lanes_of(p)].astype(BF16)
            m_ref[rows_of(b), lanes_of(p)] += mm(
                jnp.concatenate(kernels, axis=1), pair_diagonal(tile)
            )
            return carry

        lax.fori_loop(0, heads // 2, pair, 0)
        return carry

    lax.fori_loop(0, blocks, mix, 0)


def forward_mix(x, gain, wb, cw, cb, dtb, alog, skip, fcd_t):
    tokens, width = x.shape
    channels = cb.shape[1]
    heads = alog.shape[0]
    state = Q // 2
    inner = channels - 2 * state
    blocks = tokens // Q
    return pl.pallas_call(
        forward_mix_kernel,
        name="forward_mix",
        out_shape=(
            jax.ShapeDtypeStruct((tokens, width), BF16),
            jax.ShapeDtypeStruct((tokens + 8, channels), F32),
            jax.ShapeDtypeStruct((2 * heads, tokens), F32),
            jax.ShapeDtypeStruct((tokens, inner), F32),
            jax.ShapeDtypeStruct((blocks, state, inner), F32),
            jax.ShapeDtypeStruct((blocks, state, inner), F32),
        ),
        scratch_shapes=[
            pltpu.VMEM((tokens, inner), F32),
            pltpu.VMEM((tokens + 16, Q), F32),
            pltpu.VMEM((3 * heads, heads * Q), BF16),
            pltpu.VMEM((3 * heads, inner), BF16),
            pltpu.VMEM((Q, heads * Q), F32),
            pltpu.VMEM((Q, heads * Q), F32),
            pltpu.VMEM((heads, Q), F32),
            pltpu.VMEM((heads, Q), F32),
        ],
        compiler_params=pltpu.CompilerParams(vmem_limit_bytes=56 * MIB),
        cost_estimate=pl.CostEstimate(
            flops=60_000_000_000, bytes_accessed=20_000_000, transcendentals=4_000_000
        ),
    )(x, gain, wb, cw, cb, dtb, alog, skip, fcd_t)


def forward_out_kernel(x_ref, u_ref, m_ref, wa_ref, g_ref, wo_ref, z_ref, hid_ref, y_ref):
    blocks = m_ref.shape[0] // Q

    def block(b, carry):
        z = mm(u_ref[rows_of(b), :], wa_ref[...])
        z_ref[rows_of(b), :] = z
        v = m_ref[rows_of(b), :] * (z / (1.0 + jnp.exp(-z)))
        scale = lax.rsqrt(jnp.mean(v * v, axis=-1, keepdims=True) + EPS)
        hid = (v * scale * g_ref[...].astype(F32)).astype(BF16)
        hid_ref[rows_of(b), :] = hid
        y_ref[rows_of(b), :] = x_ref[rows_of(b), :].astype(F32) + mm(hid, wo_ref[...])
        return carry

    lax.fori_loop(0, blocks, block, 0)


def forward_out(x, u, m, wa, gain, wo):
    tokens, width = x.shape
    inner = m.shape[1]
    return pl.pallas_call(
        forward_out_kernel,
        name="forward_out",
        out_shape=(
            jax.ShapeDtypeStruct((tokens, inner), F32),
            jax.ShapeDtypeStruct((tokens, inner), BF16),
            jax.ShapeDtypeStruct((tokens, width), F32),
        ),
        compiler_params=pltpu.CompilerParams(vmem_limit_bytes=56 * MIB),
        cost_estimate=pl.CostEstimate(
            flops=12_000_000_000, bytes_accessed=20_000_000, transcendentals=800_000
        ),
    )(x, u, m, wa, gain, wo)


def backward_out_kernel(
    g_ref, wo_ref, z_ref, m_ref, gain_ref, wa_ref, gb_ref, dm_ref, dz_ref, dn_ref, dgain_ref
):
    tokens, inner = m_ref.shape
    blocks = tokens // Q
    dgain_ref[...] = jnp.zeros((1, inner), F32)

    def block(b, carry):
        gb = g_ref[rows_of(b), :].astype(BF16)
        gb_ref[rows_of(b), :] = gb
        dhid = mm(gb, wo_ref[...], NT)
        z = z_ref[rows_of(b), :]
        m = m_ref[rows_of(b), :]
        s = sigmoid(z)
        v = m * (z * s)
        scale = lax.rsqrt(jnp.mean(v * v, axis=-1, keepdims=True) + EPS)
        dgain_ref[...] += jnp.sum(dhid * (v * scale), axis=0, keepdims=True)
        dvn = dhid * gain_ref[...].astype(F32)
        pull = jnp.mean(dvn * v, axis=-1, keepdims=True) * (scale * scale * scale)
        dv = dvn * scale - v * pull
        dm_ref[rows_of(b), :] = dv * (z * s)
        dz = (dv * m * (s * (1.0 + z * (1.0 - s)))).astype(BF16)
        dz_ref[rows_of(b), :] = dz
        dn_ref[rows_of(b), :] = mm(dz, wa_ref[...], NT)
        return carry

    lax.fori_loop(0, blocks, block, 0)


def backward_out(g, wo, z, m, gain, wa):
    tokens, width = g.shape
    inner = m.shape[1]
    return pl.pallas_call(
        backward_out_kernel,
        name="backward_out",
        out_shape=(
            jax.ShapeDtypeStruct((tokens, width), BF16),
            jax.ShapeDtypeStruct((tokens, inner), F32),
            jax.ShapeDtypeStruct((tokens, inner), BF16),
            jax.ShapeDtypeStruct((tokens, width), F32),
            jax.ShapeDtypeStruct((1, inner), F32),
        ),
        compiler_params=pltpu.CompilerParams(vmem_limit_bytes=56 * MIB),
        cost_estimate=pl.CostEstimate(
            flops=12_000_000_000, bytes_accessed=20_000_000, transcendentals=800_000
        ),
    )(g, wo, z, m, gain, wa)


def backward_mix_kernel(
    ci_ref, rawt_ref, dm_ref, s_ref, z_ref, cw_ref, cb_ref, dtb_ref, alog_ref, skip_ref, fcd_ref,
    dp_ref, dcw_ref, dcb_ref, ddtb_ref, dalog_ref, dskip_ref, dfcd_ref,
    xs_ref, bc_ref, wide_ref, narrow_ref, cola_ref, colb_ref, rowa_ref, rowb_ref,
    ds_ref, dz_ref, dx_ref, db_ref, dcd_ref, dcu_ref, dgram_ref, sums_ref, dconv_ref,
):
    tokens, inner = dm_ref.shape
    heads = alog_ref.shape[0]
    channels = cb_ref.shape[1]
    taps = cw_ref.shape[0]
    blocks = tokens // Q
    state = Q // 2
    activate(ci_ref, cw_ref, cb_ref, xs_ref, bc_ref, blocks, inner)
    spread_matrix(wide_ref, heads, Q)
    spread_matrix(narrow_ref, heads, inner // heads)
    rate_one = -jnp.exp(alog_ref[...])
    rate = jnp.concatenate([rate_one, rate_one], axis=0)
    one_hot = narrow_ref[0:heads, :]
    dalog_ref[...] = jnp.zeros_like(dalog_ref)
    ddtb_ref[...] = jnp.zeros_like(ddtb_ref)
    dskip_ref[...] = jnp.zeros_like(dskip_ref)
    dfcd_ref[...] = jnp.zeros_like(dfcd_ref)
    zero8 = jnp.zeros((8, state), F32)
    for ref in (dcd_ref, dcu_ref):
        ref[0:8, :] = zero8
        ref[tokens + 8 : tokens + 16, :] = zero8

    def wide_sum(values):
        return head_sums(one_hot, values)

    def state_grads(b, carry):
        terms = step_terms(rawt_ref[:, rows_of(b)], dtb_ref[...], rate, heads)
        ef, er, wf, wr = weights_of(terms, heads)
        dm = dm_ref[rows_of(b), :]
        _, cdn, cup = shifted_bc(bc_ref, b)
        ds_ref[b] = mm_left(cdn.T, spread(ef, narrow_ref[...]) * dm)
        own = mm_left(cup.T, spread(er, narrow_ref[...]) * dm)

        @pl.when(b == 0)
        def _():
            dz_ref[0] = own

        @pl.when(b > 0)
        def _():
            factor = jnp.broadcast_to(jnp.exp(terms["r_last"]), (heads, Q))
            dz_ref[b] = own + dz_ref[b - 1] * spread(factor, narrow_ref[...])[0:1]

        return carry

    lax.fori_loop(0, blocks, state_grads, 0)

    def earlier(i, carry):
        b = blocks - 2 - i
        terms = step_terms(rawt_ref[:, rows_of(b)], dtb_ref[...], rate, heads)
        factor = jnp.broadcast_to(jnp.exp(terms["f_last"]), (heads, Q))
        ds_ref[b] = ds_ref[b] + ds_ref[b + 1] * spread(factor, narrow_ref[...])[0:1]
        return carry

    lax.fori_loop(0, blocks - 1, earlier, 0)

    def block(b, carry):
        terms = step_terms(rawt_ref[:, rows_of(b)], dtb_ref[...], rate, heads)
        ef, er, wf, wr = weights_of(terms, heads)
        cola_ref[...] = spread(terms["row_f"], wide_ref[...])
        colb_ref[...] = spread(terms["row_r"], wide_ref[...])
        rowa_ref[...] = terms["fe"]
        rowb_ref[...] = terms["ri"]
        x = xs_ref[rows_of(b), :]
        dm = dm_ref[rows_of(b), :]
        bmat, cdn, cup = shifted_bc(bc_ref, b)

        diag = head_sums(fcd_ref[...].astype(F32), x) + skip_ref[...]
        ddiag = wide_sum(dm * x)
        dskip_ref[...] += jnp.sum(ddiag, axis=1, keepdims=True)
        dfcd_ref[...] += mm(ddiag, x)
        dx = spread(diag, narrow_ref[...]) * dm
        tall = jnp.concatenate([ddiag, jnp.zeros((Q - heads, Q), F32)], axis=0).T
        dx = dx + mm_left(tall[:, :heads], fcd_ref[...])

        zf = spread(ef, narrow_ref[...]) * dm
        rho_f = wide_sum(zf * mm_left(cdn, s_ref[b]))
        dcdn = mm(zf, s_ref[b], NT)
        zr = spread(er, narrow_ref[...]) * dm
        rho_r = wide_sum(zr * mm_left(cup, z_ref[b]))
        dcup = mm(zr, z_ref[b], NT)

        later_on = (b < blocks - 1).astype(F32)
        dsn = ds_ref[jnp.minimum(b + 1, blocks - 1)] * later_on
        wfx = spread(wf, narrow_ref[...])
        vf = mm_left(bmat, dsn)
        omega_f = wide_sum(wfx * x * vf)
        dx = dx + wfx * vf
        db = mm(wfx * x, dsn, NT)
        last_f = jnp.exp(terms["f_last"]) * jnp.sum(wide_sum(dsn * s_ref[b]), axis=1, keepdims=True)

        earlier_on = (b > 0).astype(F32)
        dzn = dz_ref[jnp.maximum(b - 1, 0)] * earlier_on
        wrx = spread(wr, narrow_ref[...])
        vr = mm_left(bmat, dzn)
        omega_r = wide_sum(wrx * x * vr)
        dx = dx + wrx * vr
        db = db + mm(wrx * x, dzn, NT)
        last_r = jnp.exp(terms["r_last"]) * jnp.sum(wide_sum(dzn * z_ref[b]), axis=1, keepdims=True)
        dx_ref[...] = dx

        s, t = iota((Q, Q), 0), iota((Q, Q), 1)
        lower = s < t
        gram = jnp.where(lower, exact(bmat, cdn, NT), exact(bmat, cup, NT))
        gram = jnp.where(s == t, 0.0, gram)
        r2, c2 = iota((Q, 2 * Q), 0), iota((Q, 2 * Q), 1)
        beside = jnp.where(c2 < Q, (r2 > c2).astype(F32), (r2 < c2 - Q).astype(F32)).astype(BF16)
        dgram_ref[...] = jnp.zeros((Q, Q), F32)

        def pair(p, carry):
            tile = xs_ref[rows_of(b), lanes_of(p)].astype(BF16)
            dpair = pair_diagonal(dm_ref[rows_of(b), lanes_of(p)].astype(BF16))
            outer = mm(tile, dpair, NT)
            kernels, weights = [], []
            grown = dgram_ref[...]
            for j in range(2):
                h = 2 * p + j
                gaps = jnp.where(
                    lower,
                    rowa_ref[pl.ds(h, 1), :] - cola_ref[:, lanes_of(h)],
                    colb_ref[:, lanes_of(h)] - rowb_ref[pl.ds(h, 1), :],
                )
                decay = jnp.exp(jnp.minimum(gaps, 60.0))
                kernels.append((gram * decay).astype(BF16))
                product = decay * outer[:, j * Q : (j + 1) * Q]
                grown = grown + product
                weights.append((gram * product).astype(BF16))
            dgram_ref[...] = grown
            dx_ref[:, lanes_of(p)] += mm(jnp.concatenate(kernels, axis=1), dpair)
            for j in range(2):
                h = 2 * p + j
                spans = mm(weights[j], beside)
                after, before = spans[:, :Q], spans[:, Q:]
                sums_ref[0, pl.ds(h, 1), :] = jnp.sum(jnp.where(s < t, after, 0.0), axis=0, keepdims=True)
                sums_ref[1, pl.ds(h, 1), :] = jnp.sum(jnp.where(s > t, before, 0.0), axis=0, keepdims=True)
                sums_ref[2, pl.ds(h, 1), :] = jnp.sum(jnp.where(s == t, after, 0.0), axis=0, keepdims=True)
                sums_ref[3, pl.ds(h, 1), :] = jnp.sum(jnp.where(s == t, before, 0.0), axis=0, keepdims=True)
            return carry

        lax.fori_loop(0, heads // 2, pair, 0)
        xs_ref[rows_of(b), :] = dx_ref[...]

        grown = dgram_ref[...]
        low = jnp.where(lower, grown, 0.0)
        high = jnp.where(s > t, grown, 0.0)
        db = db + mm_left(low, cdn) + mm_left(high, cup)
        db_ref[rows_of(b), :] = db
        dcd_ref[pl.ds(pl.multiple_of(b * Q + 8, 8), Q), :] = dcdn + mm_left(low.T, bmat)
        dcu_ref[pl.ds(pl.multiple_of(b * Q + 8, 8), Q), :] = dcup + mm_left(high.T, bmat)

        r, c = iota((Q, Q), 0), iota((Q, Q), 1)
        above = (r > c).astype(F32)
        below = (r < c).astype(F32)
        da_f = sums_ref[0] + exact(rho_f, above) + exact(omega_f, below) + last_f
        da_r = sums_ref[1] + exact(rho_r, below) + exact(omega_r, above) + last_r
        steps = terms["steps"]
        slope = sigmoid(terms["shifted"])
        ratio = jnp.where(steps > 0.0, slope / jnp.where(steps > 0.0, steps, 1.0), 1.0)
        direct = jnp.concatenate([sums_ref[2] + omega_f, sums_ref[3] + omega_r], axis=0)
        da = jnp.concatenate([da_f, da_r], axis=0)
        draw = direct * ratio + da * rate * slope
        ddtb_ref[...] += jnp.sum(draw, axis=1, keepdims=True)
        both = da * steps
        dalog_ref[...] += rate_one * jnp.sum(both[:heads] + both[heads:], axis=1, keepdims=True)
        padded = jnp.concatenate([draw, jnp.zeros((Q - 2 * heads, Q), F32)], axis=0)
        dp_ref[rows_of(b), channels:] = padded.T[:, : 2 * heads].astype(BF16)
        return carry

    lax.fori_loop(0, blocks, block, 0)

    dconv_ref[tokens : tokens + 8, :] = jnp.zeros((8, channels), F32)
    dcw_ref[...] = jnp.zeros_like(dcw_ref)
    dcb_ref[...] = jnp.zeros_like(dcb_ref)
    tiles = inner // Q

    def pull_tile(b, j, dact):
        v = conv_tile(ci_ref, cw_ref, cb_ref, b, j)
        s = sigmoid(v)
        dconv = dact * (s * (1.0 + v * (1.0 - s)))
        dconv_ref[rows_of(b), lanes_of(j)] = dconv
        dcb_ref[:, lanes_of(j)] += jnp.sum(dconv, axis=0, keepdims=True)
        window = ci_ref[rows_of(b, Q + 8), lanes_of(j)]
        for k in range(taps):
            start = 8 - (taps - 1) + k
            dcw_ref[k : k + 1, lanes_of(j)] += jnp.sum(
                dconv * window[start : start + Q], axis=0, keepdims=True
            )

    def pull_block(b, carry):
        def tile(j, carry):
            pull_tile(b, j, xs_ref[rows_of(b), lanes_of(j)])
            return carry

        lax.fori_loop(0, tiles, tile, 0)
        down = dcd_ref[rows_of(b, Q + 16), :]
        up = dcu_ref[rows_of(b, Q + 16), :]
        dc = down[9 : 9 + Q] + up[7 : 7 + Q]
        pull_tile(b, tiles, jnp.concatenate([db_ref[rows_of(b), :], dc], axis=1))
        return carry

    lax.fori_loop(0, blocks, pull_block, 0)

    def spread_block(b, carry):
        def tile(j, carry):
            window = dconv_ref[rows_of(b, Q + 8), lanes_of(j)]
            total = jnp.zeros((Q, Q), F32)
            for k in range(taps):
                start = taps - 1 - k
                total = total + cw_ref[k : k + 1, lanes_of(j)].astype(F32) * window[start : start + Q]
            dp_ref[rows_of(b), lanes_of(j)] = total.astype(BF16)
            return carry

        lax.fori_loop(0, channels // Q, tile, 0)
        return carry

    lax.fori_loop(0, blocks, spread_block, 0)


def backward_mix(ci, rawt, dm, s, z, cw, cb, dtb, alog, skip, fcd_t):
    tokens, inner = dm.shape
    channels = cb.shape[1]
    heads = alog.shape[0]
    state = Q // 2
    blocks = tokens // Q
    return pl.pallas_call(
        backward_mix_kernel,
        name="backward_mix",
        out_shape=(
            jax.ShapeDtypeStruct((tokens, channels + 2 * heads), BF16),
            jax.ShapeDtypeStruct(cw.shape, F32),
            jax.ShapeDtypeStruct((1, channels), F32),
            jax.ShapeDtypeStruct((2 * heads, 1), F32),
            jax.ShapeDtypeStruct((heads, 1), F32),
            jax.ShapeDtypeStruct((heads, 1), F32),
            jax.ShapeDtypeStruct((heads, inner), F32),
        ),
        scratch_shapes=[
            pltpu.VMEM((tokens, inner), F32),
            pltpu.VMEM((tokens + 16, Q), F32),
            pltpu.VMEM((3 * heads, heads * Q), BF16),
            pltpu.VMEM((3 * heads, inner), BF16),
            pltpu.VMEM((Q, heads * Q), F32),
            pltpu.VMEM((Q, heads * Q), F32),
            pltpu.VMEM((heads, Q), F32),
            pltpu.VMEM((heads, Q), F32),
            pltpu.VMEM((blocks, state, inner), F32),
            pltpu.VMEM((blocks, state, inner), F32),
            pltpu.VMEM((Q, inner), F32),
            pltpu.VMEM((tokens, state), F32),
            pltpu.VMEM((tokens + 16, state), F32),
            pltpu.VMEM((tokens + 16, state), F32),
            pltpu.VMEM((Q, Q), F32),
            pltpu.VMEM((4, heads, Q), F32),
            pltpu.VMEM((tokens + 8, channels), F32),
        ],
        compiler_params=pltpu.CompilerParams(vmem_limit_bytes=56 * MIB),
        cost_estimate=pl.CostEstimate(
            flops=100_000_000_000, bytes_accessed=30_000_000, transcendentals=8_000_000
        ),
    )(ci, rawt, dm, s, z, cw, cb, dtb, alog, skip, fcd_t)


def backward_norm_kernel(g_ref, x_ref, gain_ref, dn_ref, dp_ref, wb_ref, dx_ref, dgain_ref):
    tokens, width = x_ref.shape
    blocks = tokens // Q
    dgain_ref[...] = jnp.zeros((1, width), F32)

    def block(b, carry):
        dn = dn_ref[rows_of(b), :] + mm(dp_ref[rows_of(b), :], wb_ref[...], NT)
        x = x_ref[rows_of(b), :].astype(F32)
        scale = lax.rsqrt(jnp.mean(x * x, axis=-1, keepdims=True) + EPS)
        dgain_ref[...] += jnp.sum(dn * (x * scale), axis=0, keepdims=True)
        dvn = dn * gain_ref[...].astype(F32)
        pull = jnp.mean(dvn * x, axis=-1, keepdims=True) * (scale * scale * scale)
        dx_ref[rows_of(b), :] = g_ref[rows_of(b), :].astype(F32) + dvn * scale - x * pull
        return carry

    lax.fori_loop(0, blocks, block, 0)


def backward_norm(g, x, gain, dn, dp, wb):
    tokens, width = x.shape
    return pl.pallas_call(
        backward_norm_kernel,
        name="backward_norm",
        out_shape=(
            jax.ShapeDtypeStruct((tokens, width), F32),
            jax.ShapeDtypeStruct((1, width), F32),
        ),
        compiler_params=pltpu.CompilerParams(vmem_limit_bytes=56 * MIB),
        cost_estimate=pl.CostEstimate(
            flops=3_000_000_000, bytes_accessed=9_000_000, transcendentals=0
        ),
    )(g, x, gain, dn, dp, wb)


def bit_count(n):
    return n.bit_length() - 1


def gather_blocks(block, axis_name, order):
    n = lax.axis_size(axis_name)
    bits = bit_count(n)
    if n != 1 << bits:
        return lax.all_gather(block, axis_name, axis=0, tiled=False)
    me = lax.axis_index(axis_name)
    cur = block.reshape((1,) * bits + block.shape)
    for b in order(bits):
        pairs = [(i, i ^ (1 << b)) for i in range(n)]
        other = lax.ppermute(cur, axis_name, pairs)
        axis = bits - 1 - b
        cur = jnp.where(
            (me >> b) % 2 == 0,
            jnp.concatenate([cur, other], axis=axis),
            jnp.concatenate([other, cur], axis=axis),
        )
    return cur.reshape((n,) + block.shape)


def scatter_blocks(blocks, axis_name, order, wire):
    n = lax.axis_size(axis_name)
    bits = bit_count(n)
    if n != 1 << bits:
        return lax.psum_scatter(blocks, axis_name, scatter_dimension=0, tiled=False)
    me = lax.axis_index(axis_name)
    shape = blocks.shape[1:]
    cur = blocks.reshape((2,) * bits + shape)
    for b in order(bits):
        pairs = [(i, i ^ (1 << b)) for i in range(n)]
        axis = bits - 1 - b
        mine = (me >> b) % 2
        keep = lax.dynamic_slice_in_dim(cur, mine, 1, axis)
        send = lax.dynamic_slice_in_dim(cur, 1 - mine, 1, axis).astype(wire)
        cur = keep + lax.ppermute(send, axis_name, pairs).astype(F32)
    return cur.reshape(shape)


def gather_order(bits):
    return list(range(bits - 1, -1, -1))


def scatter_order(bits):
    return list(range(bits))


def wgrad(a, b):
    return lax.dot_general(a, b, TN, preferred_element_type=F32)


def shards(
    inputs, cotangent, norm_gain, in_w, conv_w, conv_b, dt_bias, a_log, skip, fc_d, inner_gain, out_w
):
    n = lax.axis_size("fsdp")
    layers = in_w.shape[0]
    inner = inner_gain.shape[1] * n
    channels = conv_b.shape[1] * n
    width = inputs.shape[1]
    heads = a_log.shape[1]
    taps = conv_w.shape[1]
    proj = in_w.shape[2]

    small = jnp.concatenate(
        [
            member.reshape(layers, -1)
            for member in (norm_gain, conv_w, conv_b, inner_gain, fc_d)
        ],
        axis=1,
    )
    sizes = [norm_gain[0].size, conv_w[0].size, conv_b[0].size, inner_gain[0].size, fc_d[0].size]
    cuts = [sum(sizes[:i]) for i in range(len(sizes) + 1)]
    small = gather_blocks(small, "fsdp", gather_order)

    full = []
    for l in range(layers):
        wb = gather_blocks(in_w[l, :, inner:], "fsdp", gather_order).reshape(width, proj - inner)
        wa = gather_blocks(in_w[l, :, :inner], "fsdp", gather_order).reshape(width, inner)
        wo = gather_blocks(out_w[l], "fsdp", gather_order).reshape(inner, width)
        parts = [small[:, l, cuts[i] : cuts[i + 1]] for i in range(len(sizes))]
        g1 = parts[0].reshape(1, width)
        cw = parts[1].reshape(n, taps, -1).transpose(1, 0, 2).reshape(taps, channels)
        cb = parts[2].reshape(1, channels)
        g2 = parts[3].reshape(1, inner)
        fcd_t = parts[4].reshape(inner, heads).T
        full.append((g1, cw, cb, g2, fcd_t, wb, wa, wo))

    current = inputs
    saved = []
    for l in range(layers):
        g1, cw, cb, g2, fcd_t, wb, wa, wo = full[l]
        heads_in = (dt_bias[l][:, None], a_log[l][:, None], skip[l][:, None])
        u, ci, rawt, m, s, z = forward_mix(current, g1, wb, cw, cb, *heads_in, fcd_t)
        gate, hid, following = forward_out(current, u, m, wa, g2, wo)
        saved.append((current, u, ci, rawt, m, s, z, gate, hid, heads_in))
        current = following
    output = current

    upstream = cotangent
    big = [None] * layers
    little = [None] * layers
    for l in reversed(range(layers)):
        g1, cw, cb, g2, fcd_t, wb, wa, wo = full[l]
        x, u, ci, rawt, m, s, z, gate, hid, heads_in = saved[l]
        gb, dm, dz, dn, dg2 = backward_out(upstream, wo, gate, m, g2, wa)
        dwo = scatter_blocks(wgrad(hid, gb).reshape(n, -1, width), "fsdp", scatter_order, BF16)
        dwa = scatter_blocks(wgrad(u, dz).reshape(n, -1, inner), "fsdp", scatter_order, BF16)
        dp, dcw, dcb, ddtb, dalog, dskip, dfcd = backward_mix(
            ci, rawt, dm, s, z, cw, cb, *heads_in, fcd_t
        )
        dwb = scatter_blocks(
            wgrad(u, dp).reshape(n, -1, proj - inner), "fsdp", scatter_order, BF16
        )
        upstream, dg1 = backward_norm(upstream, x, g1, dn, dp, wb)
        big[l] = (jnp.concatenate([dwa, dwb], axis=1), dwo)
        little[l] = jnp.concatenate(
            [
                dg1.reshape(n, -1),
                dcw.reshape(taps, n, -1).transpose(1, 0, 2).reshape(n, -1),
                dcb.reshape(n, -1),
                dg2.reshape(n, -1),
                dfcd.T.reshape(n, -1),
                jnp.broadcast_to(
                    jnp.concatenate([ddtb[:, 0], dalog[:, 0], dskip[:, 0]])[None], (n, 4 * heads)
                ),
            ],
            axis=1,
        )
    total = scatter_blocks(jnp.stack(little, axis=1), "fsdp", scatter_order, F32)
    sizes = sizes + [2 * heads, heads, heads]
    cuts = [sum(sizes[:i]) for i in range(len(sizes) + 1)]
    parts = [total[:, cuts[i] : cuts[i + 1]] for i in range(len(sizes))]
    return (
        output,
        upstream,
        parts[0],
        jnp.stack([big[l][0] for l in range(layers)]),
        parts[1].reshape(conv_w.shape),
        parts[2],
        parts[5],
        parts[6],
        parts[7],
        parts[4].reshape(fc_d.shape),
        parts[3],
        jnp.stack([big[l][1] for l in range(layers)]),
    )


def solution(mesh):
    rows = P("fsdp", None)
    second = P(None, "fsdp")
    return jax.shard_map(
        shards,
        mesh=mesh,
        in_specs=(
            rows, rows, second, P(None, "fsdp", None), P(None, None, "fsdp"), second,
            P(), P(), P(), P(None, "fsdp", None), second, P(None, "fsdp", None),
        ),
        out_specs=(
            rows, rows, second, P(None, "fsdp", None), P(None, None, "fsdp"), second,
            P(), P(), P(), P(None, "fsdp", None), second, P(None, "fsdp", None),
        ),
        check_vma=False,
    )
```

time: 2130 us -> 650 us (0.31)
  waiting for transfers between devices: 777 us -> 173 us
  matrix products: 408 us -> 20.1 us
  other arithmetic: 369 us -> 27.6 us
  Pallas kernels: 0 us -> 278 us
  local copies, waits for them, and re-layouts: 334 us -> 64 us
  blocking collectives: 208 us -> 0 us
  starting transfers between devices: 0.99 us -> 75.3 us
    reduce_scatter x4 -> x0, waiting for transfers between devices: 512 us -> none  [the longest x2 289 us: shards(): lax.psum_scatter(in_part, 'fsdp', scatter_dimension=0, tiled=True)]
    dot_general x70 -> x6, matrix products: 399 us -> 20.1 us  [wgrad(): return lax.dot_general(a, b, TN, preferred_element_type=F32)]
    pallas_call x0 -> x10, Pallas kernels: none -> 278 us  [the longest x2 133 us: backward_mix(): pl.pallas_call(backward_mix_kernel, name='backward_mix', out_shape=(jax.S...]
    unnamed x14 -> x0, waiting for transfers between devices: 266 us -> none
    ppermute x0 -> x70, waiting for transfers between devices: none -> 173 us  [the longest x35 92 us: scatter_blocks(): cur = keep + lax.ppermute(send, axis_name, pairs).astype(F32)]
    all_gather x4 -> x0, blocking collectives: 165 us -> none  [the longest x2 85 us: shards(): lax.all_gather(conv_w[number], 'fsdp', axis=1, tiled=True)]
    reduce_sum x39 -> x0, other arithmetic: 123 us -> none  [the longest x16 31 us: advance(): return (running * factor[:, None, None] + fresh, running)]
    ppermute x0 -> x70, starting transfers between devices: none -> 75.3 us  [the longest x35 40.8 us: gather_blocks(): other = lax.ppermute(cur, axis_name, pairs)]
  transfers between devices with their start and end apart: 11 -> 70, of which waited for: 7 -> 33; matrix products, arithmetic and copies ran while one was open for 26% -> 15% of each run, Pallas kernels for 0% -> 12%
where the time goes in v1:
time: 650 us; the launch traced here: 640 us
  Pallas kernels  278 us (43%)
  waiting for transfers between devices  173 us (27%)
  starting transfers between devices  75.3 us (12%)
  local copies, waits for them, and re-layouts  64 us (10%)
  other arithmetic  27.6 us (4%)
  matrix products  20.1 us (3%)
    pallas_call x2, Pallas kernels, backward_mix(): pl.pallas_call(backward_mix_kernel, name='backward_mix', out_shape=(jax.S...  133 us
    ppermute x35, waiting for transfers between devices, scatter_blocks(): cur = keep + lax.ppermute(send, axis_name, pairs).astype(F32)  92 us
    ppermute x35, waiting for transfers between devices, gather_blocks(): other = lax.ppermute(cur, axis_name, pairs)  80.7 us
    pallas_call x2, Pallas kernels, forward_mix(): pl.pallas_call(forward_mix_kernel, name='forward_mix', out_shape=(jax.Sha...  73.7 us
    ppermute x35, starting transfers between devices, gather_blocks(): other = lax.ppermute(cur, axis_name, pairs)  40.8 us
    ppermute x35, starting transfers between devices, scatter_blocks(): cur = keep + lax.ppermute(send, axis_name, pairs).astype(F32)  34.5 us
    pallas_call x2, Pallas kernels, backward_out(): pl.pallas_call(backward_out_kernel, name='backward_out', out_shape=(jax.S...  31.1 us
    pallas_call x2, Pallas kernels, forward_out(): pl.pallas_call(forward_out_kernel, name='forward_out', out_shape=(jax.Sha...  21.6 us
  transfers between devices with their start and end apart: 70, of which 33 were waited for; matrix products, arithmetic and copies ran while one was open for 15% of the time, Pallas kernels for 12%

profile of v1, /device:TPU:0, one launch (start us, length us, event | category | flops | bytes accessed | tf_op | source)
XLA Modules:
  0.0 640.3 jit_solution(3432201423968741990)
XLA Ops:
  1.6 4.1 collective-permute-start.10
  7.7 3.0 collective-permute-start.5
  13.2 2.9 collective-permute-start.20
  22.5 1.6 collective-permute-start.1
  24.2 2.1 collective-permute-done.1
  26.3 1.6 collective-permute-start.2
  28.0 2.2 collective-permute-done.2
  30.5 2.9 collective-permute-start.25
  35.6 1.9 collective-permute-start.11
  75.9 4.7 collective-permute-done.17
  82.3 4.6 collective-permute-done.32
  88.6 4.7 collective-permute-done.27
  95.1 5.6 collective-permute-done.7
  102.4 4.3 collective-permute-done.22
  109.8 12.4 %collective-permute-done.33 = bf16[2,2,2,1,1,48,768]{6,5,4,3,2,1,0:T(8,128)(2,1)S(1)} collective-permute-done((bf16[2,2,2,1,1,48,768]{6,5,4,3,2,1,0:T(8,128)(2,1)S(1)}, bf16[2,2,2,1,1,48,768]{6,5,4,3,2,1,0:T(8,128)(2,1)S(1)}, u32[]{:S(2)}, u32[]{:S(2)}) %collective-permute-start.33) | collective-permute-done | bytes 589856 | tf_op jit(solution)/shard_map/ppermute | solution.py:697
  122.4 12.4 %collective-permute-done.28 = bf16[2,2,2,1,1,24,1536]{6,5,1,0,2,4,3:T(8,128)(2,1)S(1)} collective-permute-done((bf16[2,2,2,1,1,24,1536]{6,5,1,0,2,4,3:T(8,128)(2,1)S(1)}, bf16[2,2,2,1,1,24,1536]{6,5,1,0,2,4,3:T(8,128)(2,1)S(1)}, u32[]{:S(2)}, u32[]{:S(2)}) %collective-permute-start.28) | collective-permute-done | bytes 589856 | tf_op jit(solution)/shard_map/ppermute | solution.py:697
  135.0 14.5 %collective-permute-done.8 = bf16[2,2,2,1,1,24,1712]{6,5,4,3,2,1,0:T(8,128)(2,1)S(1)} collective-permute-done((bf16[2,2,2,1,1,24,1712]{6,5,4,3,2,1,0:T(8,128)(2,1)S(1)}, bf16[2,2,2,1,1,24,1712]{6,5,4,3,2,1,0:T(8,128)(2,1)S(1)}, u32[]{:S(2)}, u32[]{:S(2)}) %collective-permute-start.8) | collective-permute-done | bytes 657440 | tf_op jit(solution)/shard_map/ppermute | solution.py:697
  149.8 10.7 %collective-permute-done.23 = bf16[2,2,2,1,1,24,1712]{6,5,1,0,2,4,3:T(8,128)(2,1)S(1)} collective-permute-done((bf16[2,2,2,1,1,24,1712]{6,5,1,0,2,4,3:T(8,128)(2,1)S(1)}, bf16[2,2,2,1,1,24,1712]{6,5,1,0,2,4,3:T(8,128)(2,1)S(1)}, u32[]{:S(2)}, u32[]{:S(2)}) %collective-permute-start.23) | collective-permute-done | bytes 657440 | tf_op jit(solution)/shard_map/ppermute | solution.py:697
  161.8 1.7 copy.211
  163.9 1.7 copy.217
  166.2 1.6 copy.244
  168.2 1.7 copy.236
  170.4 1.8 copy.196
  172.7 1.7 copy.223
  174.4 36.7 %forward_mix.2 = (bf16[512,768]{1,0:T(8,128)(2,1)}, f32[520,1664]{1,0:T(8,128)}, f32[48,512]{1,0:T(8,128)}, f32[512,1536]{1,0:T(8,128)}, f32[4,64,1536]{2,1,0:T(8,128)}, /*index=5*/f32[4,64,1536]{2,1,0:T(8,128)}) custom-call(bf16[512,768]{1,0:T(8,128)(2,1)} %x_ref.5, bf16[1,768]{1,0:T(2,128)(2,1)} %reshape_squeeze.48.g_ref.gain_ref, ...), custom_call_target="tpu_custom_call" | custom-call | flops 60000002048 | bytes 20000000 | tf_op jit(solution)/shard_map/forward_mix/pallas_call | solution.py:273
  211.1 10.6 %forward_out.2 = (f32[512,1536]{1,0:T(8,128)}, bf16[512,1536]{1,0:T(8,128)(2,1)}, f32[512,768]{1,0:T(8,128)}) custom-call(bf16[512,768]{1,0:T(8,128)(2,1)} %x_ref.5, bf16[512,768]{1,0:T(8,128)(2,1)} %get-tuple-element.58.u_ref, f32[512,1536]{1,0:T(8,128)} %get-tuple-element.59.m_ref, bf16[768,1536]{1,0:T(8,128)(2,1)} %bitcast.243, ...), custom_call_target="tpu_custom_call" | custom-call | flops 12000000000 | bytes 20000000 | tf_op jit(solution)/shard_map/forward_out/pallas_call | solution.py:320
  221.7 37.0 %forward_mix.3 = (bf16[512,768]{1,0:T(8,128)(2,1)}, f32[520,1664]{1,0:T(8,128)}, f32[48,512]{1,0:T(8,128)}, f32[512,1536]{1,0:T(8,128)}, f32[4,64,1536]{2,1,0:T(8,128)}, /*index=5*/f32[4,64,1536]{2,1,0:T(8,128)}) custom-call(f32[512,768]{1,0:T(8,128)} %get-tuple-element.60.x_ref, bf16[1,768]{1,0:T(2,128)(2,1)} %reshape_squeeze.56.g_ref.gain_ref, ...), custom_call_target="tpu_custom_call" | custom-call | flops 60000002048 | bytes 20000000 | tf_op jit(solution)/shard_map/forward_mix/pallas_call | solution.py:273
  258.7 11.0 %forward_out.3 = (f32[512,1536]{1,0:T(8,128)}, bf16[512,1536]{1,0:T(8,128)(2,1)}, f32[512,768]{1,0:T(8,128)}) custom-call(f32[512,768]{1,0:T(8,128)} %get-tuple-element.60.x_ref, bf16[512,768]{1,0:T(8,128)(2,1)} %get-tuple-element.61.u_ref, f32[512,1536]{1,0:T(8,128)} %get-tuple-element.62.m_ref, bf16[768,1536]{1,0:T(8,128)(2,1)} %bitcast.249, ...), custom_call_target="tpu_custom_call" | custom-call | flops 12000000000 | bytes 20000000 | tf_op jit(solution)/shard_map/forward_out/pallas_call | solution.py:320
  269.7 15.4 %backward_out.2 = (bf16[512,768]{1,0:T(8,128)(2,1)}, f32[512,1536]{1,0:T(8,128)}, bf16[512,1536]{1,0:T(8,128)(2,1)}, f32[512,768]{1,0:T(8,128)}, f32[1,1536]{1,0:T(1,128)}) custom-call(bf16[512,768]{1,0:T(8,128)(2,1)} %g_ref.3, bf16[1536,768]{1,0:T(8,128)(2,1)} %bitcast.248, f32[512,1536]{1,0:T(8,128)} %get-tuple-element.64.z_ref, ...), custom_call_target="tpu_custom_call" | custom-call | flops 12000000000 | bytes 20000000 | tf_op jit(solution)/shard_map/backward_out/pallas_call | solution.py:367
  285.1 66.6 %backward_mix.2 = (bf16[512,1712]{1,0:T(8,128)(2,1)}, f32[4,1664]{1,0:T(4,128)}, f32[1,1664]{1,0:T(1,128)}, f32[48,1]{1,0:T(8,128)}, f32[24,1]{1,0:T(8,128)}, /*index=5*/f32[24,1]{1,0:T(8,128)}, f32[24,1536]{1,0:T(8,128)}) custom-call(f32[520,1664]{1,0:T(8,128)} %get-tuple-element.66.ci_ref, f32[48,512]{1,0:T(8,128)} %get-tuple-element.67.rawt_ref, ...), custom_call_target="tpu_custom_call" | custom-call | flops 99999997952 | bytes 30000000 | tf_op jit(solution)/shard_map/backward_mix/pallas_call | solution.py:612
  351.7 5.5 fusion.46
  357.2 9.4 %backward_norm.2 = (f32[512,768]{1,0:T(8,128)}, f32[1,768]{1,0:T(1,128)}) custom-call(bf16[512,768]{1,0:T(8,128)(2,1)} %g_ref.3, f32[512,768]{1,0:T(8,128)} %get-tuple-element.60.x_ref, bf16[1,768]{1,0:T(2,128)(2,1)} %reshape_squeeze.56.g_ref.gain_ref, f32[512,768]{1,0:T(8,128)} %get-tuple-element.65.dn_ref, bf16[512,1712]{1,0:T(8,128)(2,1)} %get-tuple-element.71.dp_ref, ...), custom_call_target="tpu_custom_call" | custom-call | flops 3000000000 | bytes 9000000 | tf_op jit(solution)/shard_map/backward_norm/pallas_call | solution.py:670
  366.6 15.7 %backward_out.3 = (bf16[512,768]{1,0:T(8,128)(2,1)}, f32[512,1536]{1,0:T(8,128)}, bf16[512,1536]{1,0:T(8,128)(2,1)}, f32[512,768]{1,0:T(8,128)}, f32[1,1536]{1,0:T(1,128)}) custom-call(f32[512,768]{1,0:T(8,128)} %get-tuple-element.72.g_ref, bf16[1536,768]{1,0:T(8,128)(2,1)} %bitcast.246, f32[512,1536]{1,0:T(8,128)} %get-tuple-element.73.z_ref, ...), custom_call_target="tpu_custom_call" | custom-call | flops 12000000000 | bytes 20000000 | tf_op jit(solution)/shard_map/backward_out/pallas_call | solution.py:367
  382.3 2.6 fusion.47
  391.4 1.7 copy-done.8
  393.1 3.6 fusion.43
  396.7 66.1 %backward_mix.3 = (bf16[512,1712]{1,0:T(8,128)(2,1)}, f32[4,1664]{1,0:T(4,128)}, f32[1,1664]{1,0:T(1,128)}, f32[48,1]{1,0:T(8,128)}, f32[24,1]{1,0:T(8,128)}, /*index=5*/f32[24,1]{1,0:T(8,128)}, f32[24,1536]{1,0:T(8,128)}) custom-call(f32[520,1664]{1,0:T(8,128)} %get-tuple-element.75.ci_ref, f32[48,512]{1,0:T(8,128)} %get-tuple-element.76.rawt_ref, ...), custom_call_target="tpu_custom_call" | custom-call | flops 99999997952 | bytes 30000000 | tf_op jit(solution)/shard_map/backward_mix/pallas_call | solution.py:612
  462.8 5.6 fusion.44
  470.6 9.6 %backward_norm.3 = (f32[512,768]{1,0:T(8,128)}, f32[1,768]{1,0:T(1,128)}) custom-call(f32[512,768]{1,0:T(8,128)} %get-tuple-element.72.g_ref, bf16[512,768]{1,0:T(8,128)(2,1)} %x_ref.5, bf16[1,768]{1,0:T(2,128)(2,1)} %reshape_squeeze.48.g_ref.gain_ref, f32[512,768]{1,0:T(8,128)} %get-tuple-element.74.dn_ref, bf16[512,1712]{1,0:T(8,128)(2,1)} %get-tuple-element.80.dp_ref, ...), custom_call_target="tpu_custom_call" | custom-call | flops 3000000000 | bytes 9000000 | tf_op jit(solution)/shard_map/backward_norm/pallas_call | solution.py:670
  483.9 2.9 dynamic-slice_convert_fusion.5
  489.2 3.1 dynamic-slice_convert_fusion.1
  501.0 2.0 collective-permute-start.39
  503.0 3.0 dynamic-slice_convert_fusion
  510.1 2.5 convert_add_fusion.3
  514.3 2.3 convert_add_fusion.2
  517.3 2.0 convert_add_fusion.5
  520.6 1.8 convert_add_fusion.4
  525.6 3.5 collective-permute-done.61
  530.7 11.0 %collective-permute-done.66 = bf16[2,2,2,1,1,48,768]{6,5,4,3,2,1,0:T(8,128)(2,1)S(1)} collective-permute-done((bf16[2,2,2,1,1,48,768]{6,5,4,3,2,1,0:T(8,128)(2,1)S(1)}, bf16[2,2,2,1,1,48,768]{6,5,4,3,2,1,0:T(8,128)(2,1)S(1)}, u32[]{:S(2)}, u32[]{:S(2)}) %collective-permute-start.66) | collective-permute-done | bytes 589856 | tf_op jit(solution)/shard_map/ppermute | solution.py:721
  543.4 10.9 %collective-permute-done.41 = bf16[2,2,2,1,1,24,1536]{6,5,4,3,2,1,0:T(8,128)(2,1)S(1)} collective-permute-done((bf16[2,2,2,1,1,24,1536]{6,5,4,3,2,1,0:T(8,128)(2,1)S(1)}, bf16[2,2,2,1,1,24,1536]{6,5,4,3,2,1,0:T(8,128)(2,1)S(1)}, u32[]{:S(2)}, u32[]{:S(2)}) %collective-permute-start.41) | collective-permute-done | bytes 589856 | tf_op jit(solution)/shard_map/ppermute | solution.py:721
  556.0 10.9 %collective-permute-done.51 = bf16[2,2,2,1,1,24,1536]{6,5,4,3,2,1,0:T(8,128)(2,1)S(1)} collective-permute-done((bf16[2,2,2,1,1,24,1536]{6,5,4,3,2,1,0:T(8,128)(2,1)S(1)}, bf16[2,2,2,1,1,24,1536]{6,5,4,3,2,1,0:T(8,128)(2,1)S(1)}, u32[]{:S(2)}, u32[]{:S(2)}) %collective-permute-start.51) | collective-permute-done | bytes 589856 | tf_op jit(solution)/shard_map/ppermute | solution.py:721
  568.7 13.0 %collective-permute-done.46 = bf16[2,2,2,1,1,24,1712]{6,5,4,3,2,1,0:T(8,128)(2,1)S(1)} collective-permute-done((bf16[2,2,2,1,1,24,1712]{6,5,4,3,2,1,0:T(8,128)(2,1)S(1)}, bf16[2,2,2,1,1,24,1712]{6,5,4,3,2,1,0:T(8,128)(2,1)S(1)}, u32[]{:S(2)}, u32[]{:S(2)}) %collective-permute-start.46) | collective-permute-done | bytes 657440 | tf_op jit(solution)/shard_map/ppermute | solution.py:721
  583.4 12.0 %collective-permute-done.56 = bf16[2,2,2,1,1,24,1712]{6,5,4,3,2,1,0:T(8,128)(2,1)S(1)} collective-permute-done((bf16[2,2,2,1,1,24,1712]{6,5,4,3,2,1,0:T(8,128)(2,1)S(1)}, bf16[2,2,2,1,1,24,1712]{6,5,4,3,2,1,0:T(8,128)(2,1)S(1)}, u32[]{:S(2)}, u32[]{:S(2)}) %collective-permute-start.56) | collective-permute-done | bytes 657440 | tf_op jit(solution)/shard_map/ppermute | solution.py:721
  601.1 3.5 collective-permute-done.63
  605.5 3.1 collective-permute-done.68
  609.4 2.1 collective-permute-done.43
  613.3 2.3 collective-permute-start.44
  616.5 3.3 collective-permute-done.69
  619.9 1.9 collective-permute-done.44
  623.0 2.1 collective-permute-start.58
  625.0 5.2 collective-permute-done.48
  630.5 2.1 collective-permute-done.58
  633.4 3.6 collective-permute-done.49
  637.0 1.9 collective-permute-done.59
  (385 shorter events, 122.1 us)
Async XLA Ops:
  1.6 28.9 %collective-permute-start.10 = (bf16[1,1,1,1,1,24,1536]{6,5,4,3,2,1,0:T(8,128)(2,1)S(1)}, bf16[1,1,1,1,1,24,1536]{6,5,4,3,2,1,0:T(8,128)(2,1)S(1)}, u32[]{:S(2)}, u32[]{:S(2)}) collective-permute-start(bf16[1,1,1,1,1,24,1536]{6,5,4,3,2,1,0:T(8,128)(2,1)S(1)} %get-tuple-element.141), channel_id=1, source_target_pairs={{0,16},{1,17},{2,18},{3,19},{4,20},{5,21},{6,22},{7,23},{8,24},{9,... | collective-permute-start | bytes 221192 | tf_op jit(solution)/shard_map/ppermute | solution.py:697
  6.6 27.5 %collective-permute-start.15 = (bf16[1,1,1,1,1,48,768]{6,5,4,3,2,1,0:T(8,128)(2,1)S(1)}, bf16[1,1,1,1,1,48,768]{6,5,4,3,2,1,0:T(8,128)(2,1)S(1)}, u32[]{:S(2)}, u32[]{:S(2)}) collective-permute-start(bf16[1,1,1,1,1,48,768]{6,5,4,3,2,1,0:T(8,128)(2,1)S(1)} %get-tuple-element.167), channel_id=1, source_target_pairs={{0,16},{1,17},{2,18},{3,19},{4,20},{5,21},{6,22},{7,23},{8,24},{9,... | collective-permute-start | bytes 221192 | tf_op jit(solution)/shard_map/ppermute | solution.py:697
  7.7 32.8 %collective-permute-start.5 = (bf16[1,1,1,1,1,24,1712]{6,5,4,3,2,1,0:T(8,128)(2,1)S(1)}, bf16[1,1,1,1,1,24,1712]{6,5,4,3,2,1,0:T(8,128)(2,1)S(1)}, u32[]{:S(2)}, u32[]{:S(2)}) collective-permute-start(bf16[1,1,1,1,1,24,1712]{6,5,4,3,2,1,0:T(8,128)(2,1)S(1)} %get-tuple-element.145), channel_id=1, source_target_pairs={{0,16},{1,17},{2,18},{3,19},{4,20},{5,21},{6,22},{7,23},{8,24},{9,... | collective-permute-start | bytes 246536 | tf_op jit(solution)/shard_map/ppermute | solution.py:697
  13.1 9.4 %collective-permute-start = (bf16[1,1,1,1,1,2,1484]{6,5,4,3,2,1,0:T(2,128)(2,1)S(1)}, bf16[1,1,1,1,1,2,1484]{6,5,4,3,2,1,0:T(2,128)(2,1)S(1)}, u32[]{:S(2)}, u32[]{:S(2)}) collective-permute-start(bf16[1,1,1,1,1,2,1484]{6,5,4,3,2,1,0:T(2,128)(2,1)S(1)} %bitcast.284), channel_id=1, source_target_pairs={{0,16},{1,17},{2,18},{3,19},{4,20},{5,21},{6,22},{7,23},{8,24},{9,... | collective-permute-start | bytes 17816 | tf_op jit(solution)/shard_map/ppermute | solution.py:697
  13.2 28.5 %collective-permute-start.20 = (bf16[1,1,1,1,1,24,1712]{6,5,4,3,2,1,0:T(8,128)(2,1)S(1)}, bf16[1,1,1,1,1,24,1712]{6,5,4,3,2,1,0:T(8,128)(2,1)S(1)}, u32[]{:S(2)}, u32[]{:S(2)}) collective-permute-start(bf16[1,1,1,1,1,24,1712]{6,5,4,3,2,1,0:T(8,128)(2,1)S(1)} %get-tuple-element.146), channel_id=1, source_target_pairs={{0,16},{1,17},{2,18},{3,19},{4,20},{5,21},{6,22},{7,23},{8,24},{9,... | collective-permute-start | bytes 246536 | tf_op jit(solution)/shard_map/ppermute | solution.py:697
  30.2 5.4 collective-permute-start.30
  30.5 7.8 %collective-permute-start.25 = (bf16[1,1,1,1,1,24,1536]{6,5,4,3,2,1,0:T(8,128)(2,1)S(1)}, bf16[1,1,1,1,1,24,1536]{6,5,4,3,2,1,0:T(8,128)(2,1)S(1)}, u32[]{:S(2)}, u32[]{:S(2)}) collective-permute-start(bf16[1,1,1,1,1,24,1536]{6,5,4,3,2,1,0:T(8,128)(2,1)S(1)} %get-tuple-element.142), channel_id=1, source_target_pairs={{0,16},{1,17},{2,18},{3,19},{4,20},{5,21},{6,22},{7,23},{8,24},{9,... | collective-permute-start | bytes 221192 | tf_op jit(solution)/shard_map/ppermute | solution.py:697
  34.1 9.3 %collective-permute-start.3 = (bf16[2,2,2,1,1,2,1484]{6,5,4,3,2,1,0:T(2,128)(2,1)S(1)}, bf16[2,2,2,1,1,2,1484]{6,5,4,3,2,1,0:T(2,128)(2,1)S(1)}, u32[]{:S(2)}, u32[]{:S(2)}) collective-permute-start(bf16[2,2,2,1,1,2,1484]{6,5,4,3,2,1,0:T(2,128)(2,1)S(1)} %broadcast_select_fusion.2), channel_id=1, source_target_pairs={{0,2},{1,3},{2,0},{3,1},{4,6},{5,7},{6,4},{7,5},{8,10},{9,11},{10,... | collective-permute-start | bytes 142472 | tf_op jit(solution)/shard_map/ppermute | solution.py:697
  35.6 27.7 %collective-permute-start.11 = (bf16[2,1,1,1,1,24,1536]{6,5,4,3,2,1,0:T(8,128)(2,1)}, bf16[2,1,1,1,1,24,1536]{6,5,4,3,2,1,0:T(8,128)(2,1)S(1)}, u32[]{:S(2)}, u32[]{:S(2)}) collective-permute-start(bf16[2,1,1,1,1,24,1536]{6,5,4,3,2,1,0:T(8,128)(2,1)} %maximum_select_fusion.41), channel_id=1, source_target_pairs={{0,8},{1,9},{2,10},{3,11},{4,12},{5,13},{6,14},{7,15},{8,0},{9,1},... | collective-permute-start | bytes 442376 | tf_op jit(solution)/shard_map/ppermute | solution.py:697
  38.2 26.1 %collective-permute-start.16 = (bf16[2,1,1,1,1,48,768]{6,5,0,4,3,2,1:T(8,128)(2,1)}, bf16[2,1,1,1,1,48,768]{6,5,0,4,3,2,1:T(8,128)(2,1)S(1)}, u32[]{:S(2)}, u32[]{:S(2)}) collective-permute-start(bf16[2,1,1,1,1,48,768]{6,5,0,4,3,2,1:T(8,128)(2,1)} %fusion.10), channel_id=1, source_target_pairs={{0,8},{1,9},{2,10},{3,11},{4,12},{5,13},{6,14},{7,15},{8,0},{9,1},... | collective-permute-start | bytes 442376 | tf_op jit(solution)/shard_map/ppermute | solution.py:697
  40.5 25.5 %collective-permute-start.31 = (bf16[2,1,1,1,1,48,768]{6,5,4,3,2,1,0:T(8,128)(2,1)}, bf16[2,1,1,1,1,48,768]{6,5,4,3,2,1,0:T(8,128)(2,1)S(1)}, u32[]{:S(2)}, u32[]{:S(2)}) collective-permute-start(bf16[2,1,1,1,1,48,768]{6,5,4,3,2,1,0:T(8,128)(2,1)} %maximum_select_fusion.47), channel_id=1, source_target_pairs={{0,8},{1,9},{2,10},{3,11},{4,12},{5,13},{6,14},{7,15},{8,0},{9,1},... | collective-permute-start | bytes 442376 | tf_op jit(solution)/shard_map/ppermute | solution.py:697
  41.7 24.9 %collective-permute-start.26 = (bf16[2,1,1,1,1,24,1536]{6,5,0,4,3,2,1:T(8,128)(2,1)}, bf16[2,1,1,1,1,24,1536]{6,5,0,4,3,2,1:T(8,128)(2,1)}, u32[]{:S(2)}, u32[]{:S(2)}) collective-permute-start(bf16[2,1,1,1,1,24,1536]{6,5,0,4,3,2,1:T(8,128)(2,1)} %fusion.11), channel_id=1, source_target_pairs={{0,8},{1,9},{2,10},{3,11},{4,12},{5,13},{6,14},{7,15},{8,0},{9,1},... | collective-permute-start | bytes 442376 | tf_op jit(solution)/shard_map/ppermute | solution.py:697
  44.9 25.6 %collective-permute-start.6 = (bf16[2,1,1,1,1,24,1712]{6,5,4,3,2,1,0:T(8,128)(2,1)}, bf16[2,1,1,1,1,24,1712]{6,5,4,3,2,1,0:T(8,128)(2,1)S(1)}, u32[]{:S(2)}, u32[]{:S(2)}) collective-permute-start(bf16[2,1,1,1,1,24,1712]{6,5,4,3,2,1,0:T(8,128)(2,1)} %maximum_select_fusion.37), channel_id=1, source_target_pairs={{0,8},{1,9},{2,10},{3,11},{4,12},{5,13},{6,14},{7,15},{8,0},{9,1},... | collective-permute-start | bytes 493064 | tf_op jit(solution)/shard_map/ppermute | solution.py:697
  63.3 7.8 %collective-permute-start.21 = (bf16[2,1,1,1,1,24,1712]{6,5,0,4,3,2,1:T(8,128)(2,1)}, bf16[2,1,1,1,1,24,1712]{6,5,0,4,3,2,1:T(8,128)(2,1)S(1)}, u32[]{:S(2)}, u32[]{:S(2)}) collective-permute-start(bf16[2,1,1,1,1,24,1712]{6,5,0,4,3,2,1:T(8,128)(2,1)} %fusion.9), channel_id=1, source_target_pairs={{0,8},{1,9},{2,10},{3,11},{4,12},{5,13},{6,14},{7,15},{8,0},{9,1},... | collective-permute-start | bytes 493064 | tf_op jit(solution)/shard_map/ppermute | solution.py:697
  64.3 10.0 %collective-permute-start.12 = (bf16[2,2,1,1,1,24,1536]{6,5,4,3,2,1,0:T(8,128)(2,1)S(1)}, bf16[2,2,1,1,1,24,1536]{6,5,4,3,2,1,0:T(8,128)(2,1)S(1)}, u32[]{:S(2)}, u32[]{:S(2)}) collective-permute-start(bf16[2,2,1,1,1,24,1536]{6,5,4,3,2,1,0:T(8,128)(2,1)S(1)} %maximum_select_fusion.29), channel_id=1, source_target_pairs={{0,4},{1,5},{2,6},{3,7},{4,0},{5,1},{6,2},{7,3},{8,12},{9,13},{10,... | collective-permute-start | bytes 884744 | tf_op jit(solution)/shard_map/ppermute | solution.py:697
  66.0 14.7 %collective-permute-start.17 = (bf16[2,2,1,1,1,48,768]{6,5,1,0,2,4,3:T(8,128)(2,1)S(1)}, bf16[2,2,1,1,1,48,768]{6,5,1,0,2,4,3:T(8,128)(2,1)S(1)}, u32[]{:S(2)}, u32[]{:S(2)}) collective-permute-start(bf16[2,2,1,1,1,48,768]{6,5,1,0,2,4,3:T(8,128)(2,1)S(1)} %copy.215), channel_id=1, source_target_pairs={{0,4},{1,5},{2,6},{3,7},{4,0},{5,1},{6,2},{7,3},{8,12},{9,13},{10,... | collective-permute-start | bytes 884744 | tf_op jit(solution)/shard_map/ppermute | solution.py:697
  66.7 20.3 %collective-permute-start.32 = (bf16[2,2,1,1,1,48,768]{6,5,4,3,2,1,0:T(8,128)(2,1)S(1)}, bf16[2,2,1,1,1,48,768]{6,5,4,3,2,1,0:T(8,128)(2,1)S(1)}, u32[]{:S(2)}, u32[]{:S(2)}) collective-permute-start(bf16[2,2,1,1,1,48,768]{6,5,4,3,2,1,0:T(8,128)(2,1)S(1)} %maximum_select_fusion.35), channel_id=1, source_target_pairs={{0,4},{1,5},{2,6},{3,7},{4,0},{5,1},{6,2},{7,3},{8,12},{9,13},{10,... | collective-permute-start | bytes 884744 | tf_op jit(solution)/shard_map/ppermute | solution.py:697
  70.5 22.8 %collective-permute-start.27 = (bf16[2,2,1,1,1,24,1536]{6,5,1,0,2,4,3:T(8,128)(2,1)S(1)}, bf16[2,2,1,1,1,24,1536]{6,5,1,0,2,4,3:T(8,128)(2,1)S(1)}, u32[]{:S(2)}, u32[]{:S(2)}) collective-permute-start(bf16[2,2,1,1,1,24,1536]{6,5,1,0,2,4,3:T(8,128)(2,1)S(1)} %copy.234), channel_id=1, source_target_pairs={{0,4},{1,5},{2,6},{3,7},{4,0},{5,1},{6,2},{7,3},{8,12},{9,13},{10,... | collective-permute-start | bytes 884744 | tf_op jit(solution)/shard_map/ppermute | solution.py:697
  71.2 29.5 %collective-permute-start.7 = (bf16[2,2,1,1,1,24,1712]{6,5,4,3,2,1,0:T(8,128)(2,1)S(1)}, bf16[2,2,1,1,1,24,1712]{6,5,4,3,2,1,0:T(8,128)(2,1)S(1)}, u32[]{:S(2)}, u32[]{:S(2)}) collective-permute-start(bf16[2,2,1,1,1,24,1712]{6,5,4,3,2,1,0:T(8,128)(2,1)S(1)} %maximum_select_fusion.25), channel_id=1, source_target_pairs={{0,4},{1,5},{2,6},{3,7},{4,0},{5,1},{6,2},{7,3},{8,12},{9,13},{10,... | collective-permute-start | bytes 986120 | tf_op jit(solution)/shard_map/ppermute | solution.py:697
  74.3 32.3 %collective-permute-start.22 = (bf16[2,2,1,1,1,24,1712]{6,5,1,0,2,4,3:T(8,128)(2,1)S(1)}, bf16[2,2,1,1,1,24,1712]{6,5,1,0,2,4,3:T(8,128)(2,1)S(1)}, u32[]{:S(2)}, u32[]{:S(2)}) collective-permute-start(bf16[2,2,1,1,1,24,1712]{6,5,1,0,2,4,3:T(8,128)(2,1)S(1)} %copy.221), channel_id=1, source_target_pairs={{0,4},{1,5},{2,6},{3,7},{4,0},{5,1},{6,2},{7,3},{8,12},{9,13},{10,... | collective-permute-start | bytes 986120 | tf_op jit(solution)/shard_map/ppermute | solution.py:697
  80.7 27.7 %collective-permute-start.13 = (bf16[2,2,2,1,1,24,1536]{6,5,4,3,2,1,0:T(8,128)(2,1)S(1)}, bf16[2,2,2,1,1,24,1536]{6,5,4,3,2,1,0:T(8,128)(2,1)S(1)}, u32[]{:S(2)}, u32[]{:S(2)}) collective-permute-start(bf16[2,2,2,1,1,24,1536]{6,5,4,3,2,1,0:T(8,128)(2,1)S(1)} %maximum_select_fusion.17), channel_id=1, source_target_pairs={{0,2},{1,3},{2,0},{3,1},{4,6},{5,7},{6,4},{7,5},{8,10},{9,11},{10,... | collective-permute-start | bytes 1769480 | tf_op jit(solution)/shard_map/ppermute | solution.py:697
  87.0 22.6 %collective-permute-start.18 = (bf16[2,2,2,1,1,48,768]{6,5,1,0,2,4,3:T(8,128)(2,1)S(1)}, bf16[2,2,2,1,1,48,768]{6,5,1,0,2,4,3:T(8,128)(2,1)S(1)}, u32[]{:S(2)}, u32[]{:S(2)}) collective-permute-start(bf16[2,2,2,1,1,48,768]{6,5,1,0,2,4,3:T(8,128)(2,1)S(1)} %maximum_select_fusion.19), channel_id=1, source_target_pairs={{0,2},{1,3},{2,0},{3,1},{4,6},{5,7},{6,4},{7,5},{8,10},{9,11},{10,... | collective-permute-start | bytes 1769480 | tf_op jit(solution)/shard_map/ppermute | solution.py:697
  93.3 28.9 %collective-permute-start.33 = (bf16[2,2,2,1,1,48,768]{6,5,4,3,2,1,0:T(8,128)(2,1)S(1)}, bf16[2,2,2,1,1,48,768]{6,5,4,3,2,1,0:T(8,128)(2,1)S(1)}, u32[]{:S(2)}, u32[]{:S(2)}) collective-permute-start(bf16[2,2,2,1,1,48,768]{6,5,4,3,2,1,0:T(8,128)(2,1)S(1)} %maximum_select_fusion.23), channel_id=1, source_target_pairs={{0,2},{1,3},{2,0},{3,1},{4,6},{5,7},{6,4},{7,5},{8,10},{9,11},{10,... | collective-permute-start | bytes 1769480 | tf_op jit(solution)/shard_map/ppermute | solution.py:697
  100.7 34.2 %collective-permute-start.28 = (bf16[2,2,2,1,1,24,1536]{6,5,1,0,2,4,3:T(8,128)(2,1)S(1)}, bf16[2,2,2,1,1,24,1536]{6,5,1,0,2,4,3:T(8,128)(2,1)S(1)}, u32[]{:S(2)}, u32[]{:S(2)}) collective-permute-start(bf16[2,2,2,1,1,24,1536]{6,5,1,0,2,4,3:T(8,128)(2,1)S(1)} %maximum_select_fusion.21), channel_id=1, source_target_pairs={{0,2},{1,3},{2,0},{3,1},{4,6},{5,7},{6,4},{7,5},{8,10},{9,11},{10,... | collective-permute-start | bytes 1769480 | tf_op jit(solution)/shard_map/ppermute | solution.py:697
  106.6 43.0 %collective-permute-start.8 = (bf16[2,2,2,1,1,24,1712]{6,5,4,3,2,1,0:T(8,128)(2,1)S(1)}, bf16[2,2,2,1,1,24,1712]{6,5,4,3,2,1,0:T(8,128)(2,1)S(1)}, u32[]{:S(2)}, u32[]{:S(2)}) collective-permute-start(bf16[2,2,2,1,1,24,1712]{6,5,4,3,2,1,0:T(8,128)(2,1)S(1)} %maximum_select_fusion.13), channel_id=1, source_target_pairs={{0,2},{1,3},{2,0},{3,1},{4,6},{5,7},{6,4},{7,5},{8,10},{9,11},{10,... | collective-permute-start | bytes 1972232 | tf_op jit(solution)/shard_map/ppermute | solution.py:697
  108.4 52.2 %collective-permute-start.23 = (bf16[2,2,2,1,1,24,1712]{6,5,1,0,2,4,3:T(8,128)(2,1)S(1)}, bf16[2,2,2,1,1,24,1712]{6,5,1,0,2,4,3:T(8,128)(2,1)S(1)}, u32[]{:S(2)}, u32[]{:S(2)}) collective-permute-start(bf16[2,2,2,1,1,24,1712]{6,5,1,0,2,4,3:T(8,128)(2,1)S(1)} %maximum_select_fusion.15), channel_id=1, source_target_pairs={{0,2},{1,3},{2,0},{3,1},{4,6},{5,7},{6,4},{7,5},{8,10},{9,11},{10,... | collective-permute-start | bytes 1972232 | tf_op jit(solution)/shard_map/ppermute | solution.py:697
  109.6 51.3 %collective-permute-start.14 = (bf16[2,2,2,2,1,24,1536]{6,5,1,0,2,4,3:T(8,128)(2,1)S(1)}, bf16[2,2,2,2,1,24,1536]{6,5,1,0,2,4,3:T(8,128)(2,1)S(1)}, u32[]{:S(2)}, u32[]{:S(2)}) collective-permute-start(bf16[2,2,2,2,1,24,1536]{6,5,1,0,2,4,3:T(8,128)(2,1)S(1)} %maximum_select_fusion.8), channel_id=1, source_target_pairs={{0,1},{1,0},{2,3},{3,2},{4,5},{5,4},{6,7},{7,6},{8,9},{9,8},{10,11... | collective-permute-start | bytes 3538952 | tf_op jit(solution)/shard_map/ppermute | solution.py:697
  122.2 41.3 %collective-permute-start.19 = (bf16[2,2,2,2,1,48,768]{6,5,1,0,2,4,3:T(8,128)(2,1)S(1)}, bf16[2,2,2,2,1,48,768]{6,5,1,0,2,4,3:T(8,128)(2,1)S(1)}, u32[]{:S(2)}, u32[]{:S(2)}) collective-permute-start(bf16[2,2,2,2,1,48,768]{6,5,1,0,2,4,3:T(8,128)(2,1)S(1)} %maximum_select_fusion.9), channel_id=1, source_target_pairs={{0,1},{1,0},{2,3},{3,2},{4,5},{5,4},{6,7},{7,6},{8,9},{9,8},{10,11... | collective-permute-start | bytes 3538952 | tf_op jit(solution)/shard_map/ppermute | solution.py:697
  134.8 30.7 %collective-permute-start.34 = (bf16[2,2,2,2,1,48,768]{6,5,1,0,2,4,3:T(8,128)(2,1)S(1)}, bf16[2,2,2,2,1,48,768]{6,5,1,0,2,4,3:T(8,128)(2,1)S(1)}, u32[]{:S(2)}, u32[]{:S(2)}) collective-permute-start(bf16[2,2,2,2,1,48,768]{6,5,1,0,2,4,3:T(8,128)(2,1)S(1)} %maximum_select_fusion.11), channel_id=1, source_target_pairs={{0,1},{1,0},{2,3},{3,2},{4,5},{5,4},{6,7},{7,6},{8,9},{9,8},{10,11... | collective-permute-start | bytes 3538952 | tf_op jit(solution)/shard_map/ppermute | solution.py:697
  149.6 18.2 %collective-permute-start.29 = (bf16[2,2,2,2,1,24,1536]{6,5,1,0,2,4,3:T(8,128)(2,1)S(1)}, bf16[2,2,2,2,1,24,1536]{6,5,1,0,2,4,3:T(8,128)(2,1)S(1)}, u32[]{:S(2)}, u32[]{:S(2)}) collective-permute-start(bf16[2,2,2,2,1,24,1536]{6,5,1,0,2,4,3:T(8,128)(2,1)S(1)} %maximum_select_fusion.10), channel_id=1, source_target_pairs={{0,1},{1,0},{2,3},{3,2},{4,5},{5,4},{6,7},{7,6},{8,9},{9,8},{10,11... | collective-permute-start | bytes 3538952 | tf_op jit(solution)/shard_map/ppermute | solution.py:697
  160.6 9.3 %collective-permute-start.9 = (bf16[2,2,2,2,1,24,1712]{6,5,1,0,2,4,3:T(8,128)(2,1)S(1)}, bf16[2,2,2,2,1,24,1712]{6,5,1,0,2,4,3:T(8,128)(2,1)S(1)}, u32[]{:S(2)}, u32[]{:S(2)}) collective-permute-start(bf16[2,2,2,2,1,24,1712]{6,5,1,0,2,4,3:T(8,128)(2,1)S(1)} %maximum_select_fusion.6), channel_id=1, source_target_pairs={{0,1},{1,0},{2,3},{3,2},{4,5},{5,4},{6,7},{7,6},{8,9},{9,8},{10,11... | collective-permute-start | bytes 3944456 | tf_op jit(solution)/shard_map/ppermute | solution.py:697
  160.8 11.3 %collective-permute-start.24 = (bf16[2,2,2,2,1,24,1712]{6,5,1,0,2,4,3:T(8,128)(2,1)S(1)}, bf16[2,2,2,2,1,24,1712]{6,5,1,0,2,4,3:T(8,128)(2,1)S(1)}, u32[]{:S(2)}, u32[]{:S(2)}) collective-permute-start(bf16[2,2,2,2,1,24,1712]{6,5,1,0,2,4,3:T(8,128)(2,1)S(1)} %maximum_select_fusion.7), channel_id=1, source_target_pairs={{0,1},{1,0},{2,3},{3,2},{4,5},{5,4},{6,7},{7,6},{8,9},{9,8},{10,11... | collective-permute-start | bytes 3944456 | tf_op jit(solution)/shard_map/ppermute | solution.py:697
  386.1 123.5 %collective-permute-start.60 = (bf16[2,2,2,2,1,48,768]{6,5,4,3,2,1,0:T(8,128)(2,1)}, bf16[2,2,2,2,1,48,768]{6,5,4,3,2,1,0:T(8,128)(2,1)}, u32[]{:S(2)}, u32[]{:S(2)}) collective-permute-start(bf16[2,2,2,2,1,48,768]{6,5,4,3,2,1,0:T(8,128)(2,1)} %dynamic-slice_convert_fusion.3), channel_id=1, source_target_pairs={{0,1},{1,0},{2,3},{3,2},{4,5},{5,4},{6,7},{7,6},{8,9},{9,8},{10,11... | collective-permute-start | bytes 3538952 | tf_op jit(solution)/shard_map/ppermute | solution.py:721
  390.9 121.9 %collective-permute-start.65 = (bf16[2,2,2,2,1,48,768]{6,5,4,3,2,1,0:T(8,128)(2,1)}, bf16[2,2,2,2,1,48,768]{6,5,4,3,2,1,0:T(8,128)(2,1)}, u32[]{:S(2)}, u32[]{:S(2)}) collective-permute-start(bf16[2,2,2,2,1,48,768]{6,5,4,3,2,1,0:T(8,128)(2,1)} %dynamic-slice_convert_fusion.2), channel_id=1, source_target_pairs={{0,1},{1,0},{2,3},{3,2},{4,5},{5,4},{6,7},{7,6},{8,9},{9,8},{10,11... | collective-permute-start | bytes 3538952 | tf_op jit(solution)/shard_map/ppermute | solution.py:721
  486.8 29.9 %collective-permute-start.40 = (bf16[2,2,2,2,1,24,1536]{6,5,4,3,2,1,0:T(8,128)(2,1)}, bf16[2,2,2,2,1,24,1536]{6,5,4,3,2,1,0:T(8,128)(2,1)}, u32[]{:S(2)}, u32[]{:S(2)}) collective-permute-start(bf16[2,2,2,2,1,24,1536]{6,5,4,3,2,1,0:T(8,128)(2,1)} %dynamic-slice_convert_fusion.5), channel_id=1, source_target_pairs={{0,1},{1,0},{2,3},{3,2},{4,5},{5,4},{6,7},{7,6},{8,9},{9,8},{10,11... | collective-permute-start | bytes 3538952 | tf_op jit(solution)/shard_map/ppermute | solution.py:721
  487.6 5.0 collective-permute-start.36
  492.3 30.2 %collective-permute-start.45 = (bf16[2,2,2,2,1,24,1712]{6,5,4,3,2,1,0:T(8,128)(2,1)}, bf16[2,2,2,2,1,24,1712]{6,5,4,3,2,1,0:T(8,128)(2,1)S(1)}, u32[]{:S(2)}, u32[]{:S(2)}) collective-permute-start(bf16[2,2,2,2,1,24,1712]{6,5,4,3,2,1,0:T(8,128)(2,1)} %dynamic-slice_convert_fusion.1), channel_id=1, source_target_pairs={{0,1},{1,0},{2,3},{3,2},{4,5},{5,4},{6,7},{7,6},{8,9},{9,8},{10,11... | collective-permute-start | bytes 3944456 | tf_op jit(solution)/shard_map/ppermute | solution.py:721
  501.0 5.1 collective-permute-start.39
  506.1 13.3 %collective-permute-start.50 = (bf16[2,2,2,2,1,24,1536]{6,5,4,3,2,1,0:T(8,128)(2,1)}, bf16[2,2,2,2,1,24,1536]{6,5,4,3,2,1,0:T(8,128)(2,1)}, u32[]{:S(2)}, u32[]{:S(2)}) collective-permute-start(bf16[2,2,2,2,1,24,1536]{6,5,4,3,2,1,0:T(8,128)(2,1)} %dynamic-slice_convert_fusion.4), channel_id=1, source_target_pairs={{0,1},{1,0},{2,3},{3,2},{4,5},{5,4},{6,7},{7,6},{8,9},{9,8},{10,11... | collective-permute-start | bytes 3538952 | tf_op jit(solution)/shard_map/ppermute | solution.py:721
  509.6 14.3 %collective-permute-start.55 = (bf16[2,2,2,2,1,24,1712]{6,5,4,3,2,1,0:T(8,128)(2,1)}, bf16[2,2,2,2,1,24,1712]{6,5,4,3,2,1,0:T(8,128)(2,1)S(1)}, u32[]{:S(2)}, u32[]{:S(2)}) collective-permute-start(bf16[2,2,2,2,1,24,1712]{6,5,4,3,2,1,0:T(8,128)(2,1)} %dynamic-slice_convert_fusion), channel_id=1, source_target_pairs={{0,1},{1,0},{2,3},{3,2},{4,5},{5,4},{6,7},{7,6},{8,9},{9,8},{10,11... | collective-permute-start | bytes 3944456 | tf_op jit(solution)/shard_map/ppermute | solution.py:721
  512.8 16.3 %collective-permute-start.61 = (bf16[2,2,2,1,1,48,768]{6,5,4,3,2,1,0:T(8,128)(2,1)S(1)}, bf16[2,2,2,1,1,48,768]{6,5,4,3,2,1,0:T(8,128)(2,1)S(1)}, u32[]{:S(2)}, u32[]{:S(2)}) collective-permute-start(bf16[2,2,2,1,1,48,768]{6,5,4,3,2,1,0:T(8,128)(2,1)S(1)} %dynamic-slice_convert_fusion.9), channel_id=1, source_target_pairs={{0,2},{1,3},{2,0},{3,1},{4,6},{5,7},{6,4},{7,5},{8,10},{9,11},{10,... | collective-permute-start | bytes 1769480 | tf_op jit(solution)/shard_map/ppermute | solution.py:721
  516.7 25.0 %collective-permute-start.66 = (bf16[2,2,2,1,1,48,768]{6,5,4,3,2,1,0:T(8,128)(2,1)S(1)}, bf16[2,2,2,1,1,48,768]{6,5,4,3,2,1,0:T(8,128)(2,1)S(1)}, u32[]{:S(2)}, u32[]{:S(2)}) collective-permute-start(bf16[2,2,2,1,1,48,768]{6,5,4,3,2,1,0:T(8,128)(2,1)S(1)} %dynamic-slice_convert_fusion.8), channel_id=1, source_target_pairs={{0,2},{1,3},{2,0},{3,1},{4,6},{5,7},{6,4},{7,5},{8,10},{9,11},{10,... | collective-permute-start | bytes 1769480 | tf_op jit(solution)/shard_map/ppermute | solution.py:721
  519.4 34.9 %collective-permute-start.41 = (bf16[2,2,2,1,1,24,1536]{6,5,4,3,2,1,0:T(8,128)(2,1)S(1)}, bf16[2,2,2,1,1,24,1536]{6,5,4,3,2,1,0:T(8,128)(2,1)S(1)}, u32[]{:S(2)}, u32[]{:S(2)}) collective-permute-start(bf16[2,2,2,1,1,24,1536]{6,5,4,3,2,1,0:T(8,128)(2,1)S(1)} %dynamic-slice_convert_fusion.11), channel_id=1, source_target_pairs={{0,2},{1,3},{2,0},{3,1},{4,6},{5,7},{6,4},{7,5},{8,10},{9,11},{10,... | collective-permute-start | bytes 1769480 | tf_op jit(solution)/shard_map/ppermute | solution.py:721
  522.6 44.4 %collective-permute-start.51 = (bf16[2,2,2,1,1,24,1536]{6,5,4,3,2,1,0:T(8,128)(2,1)S(1)}, bf16[2,2,2,1,1,24,1536]{6,5,4,3,2,1,0:T(8,128)(2,1)S(1)}, u32[]{:S(2)}, u32[]{:S(2)}) collective-permute-start(bf16[2,2,2,1,1,24,1536]{6,5,4,3,2,1,0:T(8,128)(2,1)S(1)} %dynamic-slice_convert_fusion.10), channel_id=1, source_target_pairs={{0,2},{1,3},{2,0},{3,1},{4,6},{5,7},{6,4},{7,5},{8,10},{9,11},{10,... | collective-permute-start | bytes 1769480 | tf_op jit(solution)/shard_map/ppermute | solution.py:721
  524.0 57.7 %collective-permute-start.46 = (bf16[2,2,2,1,1,24,1712]{6,5,4,3,2,1,0:T(8,128)(2,1)S(1)}, bf16[2,2,2,1,1,24,1712]{6,5,4,3,2,1,0:T(8,128)(2,1)S(1)}, u32[]{:S(2)}, u32[]{:S(2)}) collective-permute-start(bf16[2,2,2,1,1,24,1712]{6,5,4,3,2,1,0:T(8,128)(2,1)S(1)} %dynamic-slice_convert_fusion.7), channel_id=1, source_target_pairs={{0,2},{1,3},{2,0},{3,1},{4,6},{5,7},{6,4},{7,5},{8,10},{9,11},{10,... | collective-permute-start | bytes 1972232 | tf_op jit(solution)/shard_map/ppermute | solution.py:721
  529.0 66.4 %collective-permute-start.56 = (bf16[2,2,2,1,1,24,1712]{6,5,4,3,2,1,0:T(8,128)(2,1)S(1)}, bf16[2,2,2,1,1,24,1712]{6,5,4,3,2,1,0:T(8,128)(2,1)S(1)}, u32[]{:S(2)}, u32[]{:S(2)}) collective-permute-start(bf16[2,2,2,1,1,24,1712]{6,5,4,3,2,1,0:T(8,128)(2,1)S(1)} %dynamic-slice_convert_fusion.6), channel_id=1, source_target_pairs={{0,2},{1,3},{2,0},{3,1},{4,6},{5,7},{6,4},{7,5},{8,10},{9,11},{10,... | collective-permute-start | bytes 1972232 | tf_op jit(solution)/shard_map/ppermute | solution.py:721
  541.7 55.4 %collective-permute-start.62 = (bf16[2,2,1,1,1,48,768]{6,5,4,3,2,1,0:T(8,128)(2,1)S(1)}, bf16[2,2,1,1,1,48,768]{6,5,4,3,2,1,0:T(8,128)(2,1)S(1)}, u32[]{:S(2)}, u32[]{:S(2)}) collective-permute-start(bf16[2,2,1,1,1,48,768]{6,5,4,3,2,1,0:T(8,128)(2,1)S(1)} %dynamic-slice_convert_fusion.15), channel_id=1, source_target_pairs={{0,4},{1,5},{2,6},{3,7},{4,0},{5,1},{6,2},{7,3},{8,12},{9,13},{10,... | collective-permute-start | bytes 884744 | tf_op jit(solution)/shard_map/ppermute | solution.py:721
  554.3 43.5 %collective-permute-start.67 = (bf16[2,2,1,1,1,48,768]{6,5,4,3,2,1,0:T(8,128)(2,1)S(1)}, bf16[2,2,1,1,1,48,768]{6,5,4,3,2,1,0:T(8,128)(2,1)S(1)}, u32[]{:S(2)}, u32[]{:S(2)}) collective-permute-start(bf16[2,2,1,1,1,48,768]{6,5,4,3,2,1,0:T(8,128)(2,1)S(1)} %dynamic-slice_convert_fusion.14), channel_id=1, source_target_pairs={{0,4},{1,5},{2,6},{3,7},{4,0},{5,1},{6,2},{7,3},{8,12},{9,13},{10,... | collective-permute-start | bytes 884744 | tf_op jit(solution)/shard_map/ppermute | solution.py:721
  567.0 31.8 %collective-permute-start.42 = (bf16[2,2,1,1,1,24,1536]{6,5,4,3,2,1,0:T(8,128)(2,1)S(1)}, bf16[2,2,1,1,1,24,1536]{6,5,4,3,2,1,0:T(8,128)(2,1)S(1)}, u32[]{:S(2)}, u32[]{:S(2)}) collective-permute-start(bf16[2,2,1,1,1,24,1536]{6,5,4,3,2,1,0:T(8,128)(2,1)S(1)} %dynamic-slice_convert_fusion.17), channel_id=1, source_target_pairs={{0,4},{1,5},{2,6},{3,7},{4,0},{5,1},{6,2},{7,3},{8,12},{9,13},{10,... | collective-permute-start | bytes 884744 | tf_op jit(solution)/shard_map/ppermute | solution.py:721
  581.7 18.5 %collective-permute-start.52 = (bf16[2,2,1,1,1,24,1536]{6,5,4,3,2,1,0:T(8,128)(2,1)S(1)}, bf16[2,2,1,1,1,24,1536]{6,5,4,3,2,1,0:T(8,128)(2,1)S(1)}, u32[]{:S(2)}, u32[]{:S(2)}) collective-permute-start(bf16[2,2,1,1,1,24,1536]{6,5,4,3,2,1,0:T(8,128)(2,1)S(1)} %dynamic-slice_convert_fusion.16), channel_id=1, source_target_pairs={{0,4},{1,5},{2,6},{3,7},{4,0},{5,1},{6,2},{7,3},{8,12},{9,13},{10,... | collective-permute-start | bytes 884744 | tf_op jit(solution)/shard_map/ppermute | solution.py:721
  595.4 27.3 %collective-permute-start.47 = (bf16[2,2,1,1,1,24,1712]{6,5,4,3,2,1,0:T(8,128)(2,1)S(1)}, bf16[2,2,1,1,1,24,1712]{6,5,4,3,2,1,0:T(8,128)(2,1)S(1)}, u32[]{:S(2)}, u32[]{:S(2)}) collective-permute-start(bf16[2,2,1,1,1,24,1712]{6,5,4,3,2,1,0:T(8,128)(2,1)S(1)} %dynamic-slice_convert_fusion.13), channel_id=1, source_target_pairs={{0,4},{1,5},{2,6},{3,7},{4,0},{5,1},{6,2},{7,3},{8,12},{9,13},{10,... | collective-permute-start | bytes 986120 | tf_op jit(solution)/shard_map/ppermute | solution.py:721
  597.1 25.7 %collective-permute-start.57 = (bf16[2,2,1,1,1,24,1712]{6,5,4,3,2,1,0:T(8,128)(2,1)S(1)}, bf16[2,2,1,1,1,24,1712]{6,5,4,3,2,1,0:T(8,128)(2,1)S(1)}, u32[]{:S(2)}, u32[]{:S(2)}) collective-permute-start(bf16[2,2,1,1,1,24,1712]{6,5,4,3,2,1,0:T(8,128)(2,1)S(1)} %dynamic-slice_convert_fusion.12), channel_id=1, source_target_pairs={{0,4},{1,5},{2,6},{3,7},{4,0},{5,1},{6,2},{7,3},{8,12},{9,13},{10,... | collective-permute-start | bytes 986120 | tf_op jit(solution)/shard_map/ppermute | solution.py:721
  597.8 6.8 %collective-permute-start.63 = (bf16[2,1,1,1,1,48,768]{6,5,4,3,2,1,0:T(8,128)(2,1)S(1)}, bf16[2,1,1,1,1,48,768]{6,5,4,3,2,1,0:T(8,128)(2,1)S(1)}, u32[]{:S(2)}, u32[]{:S(2)}) collective-permute-start(bf16[2,1,1,1,1,48,768]{6,5,4,3,2,1,0:T(8,128)(2,1)S(1)} %dynamic-slice_convert_fusion.21), channel_id=1, source_target_pairs={{0,8},{1,9},{2,10},{3,11},{4,12},{5,13},{6,14},{7,15},{8,0},{9,1},... | collective-permute-start | bytes 442376 | tf_op jit(solution)/shard_map/ppermute | solution.py:721
  598.7 9.9 %collective-permute-start.68 = (bf16[2,1,1,1,1,48,768]{6,5,4,3,2,1,0:T(8,128)(2,1)S(1)}, bf16[2,1,1,1,1,48,768]{6,5,4,3,2,1,0:T(8,128)(2,1)S(1)}, u32[]{:S(2)}, u32[]{:S(2)}) collective-permute-start(bf16[2,1,1,1,1,48,768]{6,5,4,3,2,1,0:T(8,128)(2,1)S(1)} %dynamic-slice_convert_fusion.20), channel_id=1, source_target_pairs={{0,8},{1,9},{2,10},{3,11},{4,12},{5,13},{6,14},{7,15},{8,0},{9,1},... | collective-permute-start | bytes 442376 | tf_op jit(solution)/shard_map/ppermute | solution.py:721
  600.2 11.4 %collective-permute-start.43 = (bf16[2,1,1,1,1,24,1536]{6,5,4,3,2,1,0:T(8,128)(2,1)S(1)}, bf16[2,1,1,1,1,24,1536]{6,5,4,3,2,1,0:T(8,128)(2,1)S(1)}, u32[]{:S(2)}, u32[]{:S(2)}) collective-permute-start(bf16[2,1,1,1,1,24,1536]{6,5,4,3,2,1,0:T(8,128)(2,1)S(1)} %dynamic-slice_convert_fusion.23), channel_id=1, source_target_pairs={{0,8},{1,9},{2,10},{3,11},{4,12},{5,13},{6,14},{7,15},{8,0},{9,1},... | collective-permute-start | bytes 442376 | tf_op jit(solution)/shard_map/ppermute | solution.py:721
  604.6 8.6 %collective-permute-start.53 = (bf16[2,1,1,1,1,24,1536]{6,5,4,3,2,1,0:T(8,128)(2,1)S(1)}, bf16[2,1,1,1,1,24,1536]{6,5,4,3,2,1,0:T(8,128)(2,1)S(1)}, u32[]{:S(2)}, u32[]{:S(2)}) collective-permute-start(bf16[2,1,1,1,1,24,1536]{6,5,4,3,2,1,0:T(8,128)(2,1)S(1)} %dynamic-slice_convert_fusion.22), channel_id=1, source_target_pairs={{0,8},{1,9},{2,10},{3,11},{4,12},{5,13},{6,14},{7,15},{8,0},{9,1},... | collective-permute-start | bytes 442376 | tf_op jit(solution)/shard_map/ppermute | solution.py:721
  608.6 7.0 %collective-permute-start.64 = (bf16[1,1,1,1,1,48,768]{6,5,4,3,2,1,0:T(8,128)(2,1)S(1)}, bf16[1,1,1,1,1,48,768]{6,5,4,3,2,1,0:T(8,128)(2,1)S(1)}, u32[]{:S(2)}, u32[]{:S(2)}) collective-permute-start(bf16[1,1,1,1,1,48,768]{6,5,4,3,2,1,0:T(8,128)(2,1)S(1)} %dynamic-slice_convert_fusion.27), channel_id=1, source_target_pairs={{0,16},{1,17},{2,18},{3,19},{4,20},{5,21},{6,22},{7,23},{8,24},{9,... | collective-permute-start | bytes 221192 | tf_op jit(solution)/shard_map/ppermute | solution.py:721
  611.6 8.3 %collective-permute-start.69 = (bf16[1,1,1,1,1,48,768]{6,5,4,3,2,1,0:T(8,128)(2,1)S(1)}, bf16[1,1,1,1,1,48,768]{6,5,4,3,2,1,0:T(8,128)(2,1)S(1)}, u32[]{:S(2)}, u32[]{:S(2)}) collective-permute-start(bf16[1,1,1,1,1,48,768]{6,5,4,3,2,1,0:T(8,128)(2,1)S(1)} %dynamic-slice_convert_fusion.26), channel_id=1, source_target_pairs={{0,16},{1,17},{2,18},{3,19},{4,20},{5,21},{6,22},{7,23},{8,24},{9,... | collective-permute-start | bytes 221192 | tf_op jit(solution)/shard_map/ppermute | solution.py:721
  613.3 8.5 %collective-permute-start.44 = (bf16[1,1,1,1,1,24,1536]{6,5,4,3,2,1,0:T(8,128)(2,1)S(1)}, bf16[1,1,1,1,1,24,1536]{6,5,4,3,2,1,0:T(8,128)(2,1)S(1)}, u32[]{:S(2)}, u32[]{:S(2)}) collective-permute-start(bf16[1,1,1,1,1,24,1536]{6,5,4,3,2,1,0:T(8,128)(2,1)S(1)} %dynamic-slice_convert_fusion.29), channel_id=1, source_target_pairs={{0,16},{1,17},{2,18},{3,19},{4,20},{5,21},{6,22},{7,23},{8,24},{9,... | collective-permute-start | bytes 221192 | tf_op jit(solution)/shard_map/ppermute | solution.py:721
  615.6 7.0 %collective-permute-start.54 = (bf16[1,1,1,1,1,24,1536]{6,5,4,3,2,1,0:T(8,128)(2,1)S(1)}, bf16[1,1,1,1,1,24,1536]{6,5,4,3,2,1,0:T(8,128)(2,1)S(1)}, u32[]{:S(2)}, u32[]{:S(2)}) collective-permute-start(bf16[1,1,1,1,1,24,1536]{6,5,4,3,2,1,0:T(8,128)(2,1)S(1)} %dynamic-slice_convert_fusion.28), channel_id=1, source_target_pairs={{0,16},{1,17},{2,18},{3,19},{4,20},{5,21},{6,22},{7,23},{8,24},{9,... | collective-permute-start | bytes 221192 | tf_op jit(solution)/shard_map/ppermute | solution.py:721
  622.8 7.5 %collective-permute-start.48 = (bf16[2,1,1,1,1,24,1712]{6,5,4,3,2,1,0:T(8,128)(2,1)S(1)}, bf16[2,1,1,1,1,24,1712]{6,5,4,3,2,1,0:T(8,128)(2,1)S(1)}, u32[]{:S(2)}, u32[]{:S(2)}) collective-permute-start(bf16[2,1,1,1,1,24,1712]{6,5,4,3,2,1,0:T(8,128)(2,1)S(1)} %dynamic-slice_convert_fusion.19), channel_id=1, source_target_pairs={{0,8},{1,9},{2,10},{3,11},{4,12},{5,13},{6,14},{7,15},{8,0},{9,1},... | collective-permute-start | bytes 493064 | tf_op jit(solution)/shard_map/ppermute | solution.py:721
  623.0 9.7 %collective-permute-start.58 = (bf16[2,1,1,1,1,24,1712]{6,5,4,3,2,1,0:T(8,128)(2,1)S(1)}, bf16[2,1,1,1,1,24,1712]{6,5,4,3,2,1,0:T(8,128)(2,1)S(1)}, u32[]{:S(2)}, u32[]{:S(2)}) collective-permute-start(bf16[2,1,1,1,1,24,1712]{6,5,4,3,2,1,0:T(8,128)(2,1)S(1)} %dynamic-slice_convert_fusion.18), channel_id=1, source_target_pairs={{0,8},{1,9},{2,10},{3,11},{4,12},{5,13},{6,14},{7,15},{8,0},{9,1},... | collective-permute-start | bytes 493064 | tf_op jit(solution)/shard_map/ppermute | solution.py:721
  630.3 6.7 %collective-permute-start.49 = (bf16[1,1,1,1,1,24,1712]{6,5,4,3,2,1,0:T(8,128)(2,1)S(1)}, bf16[1,1,1,1,1,24,1712]{6,5,4,3,2,1,0:T(8,128)(2,1)S(1)}, u32[]{:S(2)}, u32[]{:S(2)}) collective-permute-start(bf16[1,1,1,1,1,24,1712]{6,5,4,3,2,1,0:T(8,128)(2,1)S(1)} %dynamic-slice_convert_fusion.25), channel_id=1, source_target_pairs={{0,16},{1,17},{2,18},{3,19},{4,20},{5,21},{6,22},{7,23},{8,24},{9,... | collective-permute-start | bytes 246536 | tf_op jit(solution)/shard_map/ppermute | solution.py:721
  632.7 6.3 collective-permute-start.59
  (39 other events, 251.0 us)
